TPU v7x, 128 devices: a whole 4x4x4 slice. The times are simulated.
128 devices in a mesh: fsdp: 4 (over z), seq: 8 (over x, core), head: 4 (over y).
Axes of the slice: x: 4, y: 4, z: 4, core: 2. Of those that a mesh axis runs over, the one named last changes fastest.
Arguments:
- queries: bfloat16 [8192, 4096], P(('fsdp', 'seq'), 'head'), may hold values from -6 to 6
- span_k: bfloat16 [8192, 512], P(('fsdp', 'seq'), 'head'), may hold values from -6 to 6
- span_v: bfloat16 [8192, 512], P(('fsdp', 'seq'), 'head'), may hold values from -6 to 6
- cache_k: bfloat16 [2048, 128, 512], P(('fsdp', 'seq'), None, 'head'), may hold values from -6 to 6
- cache_v: bfloat16 [2048, 128, 512], P(('fsdp', 'seq'), None, 'head'), may hold values from -6 to 6
- block_slot: int32 [2048], replicated, may hold values from 0 to 2047, as said below
- pattern: int32 [64, 48], P(('fsdp', 'seq')), may hold values from 0 to 2047, as said below
- wo: bfloat16 [4096, 8192], P('head', 'fsdp'), may hold values from -6 to 6
Outputs:
- mixed: bfloat16 [8192, 8192], P(('fsdp', 'seq'))
Inputs may be any that keep to these rules, and one draw needn't show every extreme that they name: `pattern`: each row lists 48 different blocks. Of the 96 entries in the rows of one index of fsdp and seq, all are different, at most 6 have a storage row block_slot between o * 64 and (o + 1) * 64 - 1 for any o, and exactly 6 do for some o. A permutation: block c is stored at row block_slot[c] of cache_k and cache_v.
All inputs are finite; a program needn't handle non-finite values.
Results may differ from a plain program's by a relative error of at most 0.0095.
Values may be sent and summed in bfloat16 or wider, within the bound.
A program may use at most 128 MiB of HBM per device.

v0:
```python
import jax
import jax.numpy as jnp
from jax import lax
from jax.sharding import PartitionSpec as P

HD = 128


def from_behind(value, axis, steps):
    count = lax.axis_size(axis)
    leading, last = (max(0, -steps), min(count, count - steps))
    return lax.ppermute(value, axis, [(source, source + steps) for source in range(leading, last)])


def attend_block(query_block, keys, values, present):
    length = keys.shape[0]
    block_len = query_block.shape[0]
    kv_local = query_block.shape[1]
    head_dim = query_block.shape[3]
    keys_four = keys.reshape(length, kv_local, head_dim)
    values_four = values.reshape(length, kv_local, head_dim)
    scores = jnp.einsum(
        "tkgd,lkd->kgtl", query_block, keys_four, preferred_element_type=jnp.float32
    ) / jnp.sqrt(jnp.float32(head_dim))
    column = jnp.arange(length)[None, :]
    row_ids = jnp.arange(block_len)[:, None]
    listed_end = length - 2 * block_len
    own_start = listed_end + block_len
    allowed = (
        (column < listed_end)
        | (column >= listed_end) & (column < own_start) & present
        | (column >= own_start) & (column - own_start <= row_ids)
    )
    scores = jnp.where(allowed, scores, -jnp.inf)
    top = jnp.max(scores, axis=-1, keepdims=True)
    expo = jnp.exp(scores - top)
    probs_bf = (expo / jnp.sum(expo, axis=-1, keepdims=True)).astype(jnp.bfloat16)
    output = jnp.einsum("kgtl,lkd->tkgd", probs_bf, values_four, preferred_element_type=jnp.float32)
    return output.reshape(block_len, -1).astype(jnp.bfloat16)


def body(queries, span_k, span_v, cache_k, cache_v, block_slot, pattern, wo):
    seq_devs = lax.axis_size(("fsdp", "seq"))
    index_here = lax.axis_index(("fsdp", "seq"))
    qb_local, list_len = pattern.shape
    cb_local, block_len, kv_cols = cache_k.shape
    kv_local = kv_cols // HD
    group_size = queries.shape[1] // kv_cols
    requests = qb_local * list_len
    capacity = max(2, 2 * requests // seq_devs)
    slot_ids = block_slot[pattern.reshape(-1)]
    owners = slot_ids // cb_local
    within = slot_ids % cb_local
    position = jnp.arange(requests)
    earlier = (owners[None, :] == owners[:, None]) & (position[None, :] < position[:, None])
    ranking = jnp.sum(earlier.astype(jnp.int32), axis=1)
    places = owners * capacity + ranking
    wanted = jnp.zeros((seq_devs * capacity,), jnp.int32).at[places].set(within)
    asked_ids = lax.all_to_all(
        wanted.reshape(seq_devs, capacity), ("fsdp", "seq"), split_axis=0, concat_axis=0, tiled=True
    ).reshape(-1)
    send_k = cache_k[asked_ids]
    send_v = cache_v[asked_ids]
    got_k, got_v = (
        lax.all_to_all(send_k, ("fsdp", "seq"), split_axis=0, concat_axis=0, tiled=True),
        lax.all_to_all(send_v, ("fsdp", "seq"), split_axis=0, concat_axis=0, tiled=True),
    )
    listed_k = got_k[places].reshape(qb_local, list_len * block_len, kv_cols)
    listed_v = got_v[places].reshape(qb_local, list_len * block_len, kv_cols)
    prev_k, prev_v = from_behind((span_k[-block_len:], span_v[-block_len:]), ("fsdp", "seq"), 1)
    own_k = span_k.reshape(qb_local, block_len, kv_cols)
    own_v = span_v.reshape(qb_local, block_len, kv_cols)
    before_k = jnp.concatenate([prev_k[None], own_k[:-1]], axis=0)
    before_v = jnp.concatenate([prev_v[None], own_v[:-1]], axis=0)
    present = index_here * qb_local + jnp.arange(qb_local) > 0
    query_blocks = queries.reshape(qb_local, block_len, kv_local, group_size, HD)

    def one_block(inputs):
        query_block, list_keys, list_values, prior_k, prior_v, self_k, self_v, flag = inputs
        keys = jnp.concatenate([list_keys, prior_k, self_k], axis=0)
        values = jnp.concatenate([list_values, prior_v, self_v], axis=0)
        return attend_block(query_block, keys, values, flag)

    attended = lax.map(
        one_block, (query_blocks, listed_k, listed_v, before_k, before_v, own_k, own_v, present)
    )
    attended = attended.reshape(qb_local * block_len, -1)
    partial_terms = jnp.dot(
        attended, lax.all_gather(wo, "fsdp", axis=1, tiled=True), preferred_element_type=jnp.float32
    )
    mixed = lax.psum(partial_terms.astype(jnp.bfloat16), "head")
    return mixed


def solution(mesh):
    return jax.shard_map(
        body,
        mesh=mesh,
        in_specs=(
            P(("fsdp", "seq"), "head"),
            P(("fsdp", "seq"), "head"),
            P(("fsdp", "seq"), "head"),
            P(("fsdp", "seq"), None, "head"),
            P(("fsdp", "seq"), None, "head"),
            P(),
            P(("fsdp", "seq"), None),
            P("head", "fsdp"),
        ),
        out_specs=P(("fsdp", "seq"), None),
        check_vma=False,
    )
```

profile of v0, /device:TPU:0, one launch (start us, length us, event | category | flops | bytes accessed | tf_op | source)
XLA Modules:
  0.0 446.3 jit_solution(8823667803559254925)
XLA Ops:
  6.5 0.9 reshape.258
  7.5 1.6 gather_fusion
  9.1 0.2 convert_reduce_fusion
  9.3 0.9 scatter_custom_fusion
  10.3 15.5 %all_to_all.19 = s32[32,1,6]{2,1,0:T(1,128)S(1)} all-to-all(s32[32,1,6]{2,1,0:T(1,128)S(1)} %bitcast.125), channel_id=1, replica_groups=mesh['fsdp'=4,'seq'=8,'head'=4] {'fsdp','seq'}, dimensions={0} | all-to-all | bytes 1536 | tf_op jit(solution)/shard_map/all_to_all | solution.py:59
  25.7 0.5 broadcast.294
  26.3 0.7 reduce.11
  27.1 8.0 %gather_fusion.1 = bf16[192,128,128]{2,1,0:T(8,128)(2,1)} fusion(bf16[64,128,128]{2,1,0:T(8,128)(2,1)S(1)} %copy-done, s32[1024]{0:T(1024)S(1)} %pad_clamp_fusion.1), kind=kCustom, calls=%fused_computation.1 | custom fusion | bytes 12583680 | tf_op jit(solution)/shard_map/gather | solution.py:63
  35.1 5.0 %all-to-all-start.1 = ((bf16[192,128,128]{2,1,0:T(8,128)(2,1)}), bf16[192,128,128]{2,1,0:T(8,128)(2,1)}, u32[]{:S(2)}, u32[]{:S(2)}) async-start(bf16[192,128,128]{2,1,0:T(8,128)(2,1)} %gather_fusion.1), calls=%async_computation.1 | async-start | bytes 12582912 | tf_op jit(solution)/shard_map/all_to_all | solution.py:66
  40.2 7.9 %gather_fusion.3 = bf16[192,128,128]{2,1,0:T(8,128)(2,1)} fusion(bf16[64,128,128]{2,1,0:T(8,128)(2,1)S(1)} %copy-done.3, s32[1024]{0:T(1024)S(1)} %pad_clamp_fusion.1), kind=kCustom, calls=%fused_computation.3 | custom fusion | bytes 12583680 | tf_op jit(solution)/shard_map/gather | solution.py:62
  48.1 69.9 %all-to-all-done.1 = bf16[192,128,128]{2,1,0:T(8,128)(2,1)} async-done(((bf16[192,128,128]{2,1,0:T(8,128)(2,1)}), bf16[192,128,128]{2,1,0:T(8,128)(2,1)}, u32[]{:S(2)}, u32[]{:S(2)}) %all-to-all-start.1) | async-done | bytes 6291488 | tf_op jit(solution)/shard_map/all_to_all | solution.py:66
  118.0 4.9 %all-to-all-start.2 = ((bf16[192,128,128]{2,1,0:T(8,128)(2,1)}), bf16[192,128,128]{2,1,0:T(8,128)(2,1)}, u32[]{:S(2)}, u32[]{:S(2)}) async-start(bf16[192,128,128]{2,1,0:T(8,128)(2,1)} %gather_fusion.3), calls=%async_computation.2 | async-start | bytes 12582912 | tf_op jit(solution)/shard_map/all_to_all | solution.py:65
  123.0 0.7 all-gather.2.cloned.1.call-update
  123.8 0.1 copy.41
  123.9 2.0 collective-permute-start
  125.9 3.7 collective-permute-start.1
  129.7 0.1 copy.42
  130.0 0.4 collective-permute-done.1
  130.3 5.5 %gather_fusion.2 = bf16[96,128,128]{2,1,0:T(8,128)(2,1)} fusion(bf16[192,128,128]{2,1,0:T(8,128)(2,1)} %all-to-all-done.1, s32[1024]{0:T(1024)S(1)} %pad_clamp_fusion), kind=kCustom, calls=%fused_computation.2 | custom fusion | bytes 6291840 | tf_op jit(solution)/shard_map/gather | solution.py:69
  135.8 73.3 %all-to-all-done.2 = bf16[192,128,128]{2,1,0:T(8,128)(2,1)} async-done(((bf16[192,128,128]{2,1,0:T(8,128)(2,1)}), bf16[192,128,128]{2,1,0:T(8,128)(2,1)}, u32[]{:S(2)}, u32[]{:S(2)}) %all-to-all-start.2) | async-done | bytes 6291488 | tf_op jit(solution)/shard_map/all_to_all | solution.py:65
  209.1 5.5 %gather_fusion.4 = bf16[96,128,128]{2,1,0:T(8,128)(2,1)} fusion(bf16[192,128,128]{2,1,0:T(8,128)(2,1)} %all-to-all-done.2, s32[1024]{0:T(1024)S(1)} %pad_clamp_fusion), kind=kCustom, calls=%fused_computation.4 | custom fusion | bytes 6291840 | tf_op jit(solution)/shard_map/gather | solution.py:68
  214.6 98.3 %while.12 = (s32[]{:T(128)}, bf16[2,128,1024]{2,1,0:T(8,128)(2,1)}, bf16[2,6144,128]{2,1,0:T(8,128)(2,1)}, bf16[2,128,128]{1,2,0:T(8,128)(2,1)S(1)}, bf16[2,128,...) while((s32[]{:T(128)}, bf16[2,128,1024]{2,1,0:T(8,128)(2,1)}, ...), condition=%wide.region_5.6_spmd, body=%wide.region_2.5_spmd.sunk | while | flops 3446554624 | bytes 113933528 | solution.py:84
  214.6 0.6 dynamic_slice.72
  215.2 0.6 iota_compare_fusion.7
  215.8 5.8 %fusion.40 = pred[128,6400]{0,1:T(8,128)(4,1)S(1)} fusion(s32[6400]{0:T(1024)S(1)} %iota_add_fusion.2, pred[6400]{0:T(1024)(128)(4,1)S(1)} %get-tuple-element.260, pred[6400]{0:T(1024)(128)(4,1)S(1)} %get-tuple-element.261), kind=kLoop, calls=%fused_computation.15.clone.1 | loop fusion | flops 2457600 | bytes 857600 | tf_op jit(solution)/shard_map/while/body/eval_jaxpr/or | solution.py:30
  221.6 1.5 dynamic-slice_bitcast_fusion.8
  223.2 13.4 %fusion.41 = (f32[8,128]{1,0:T(8,128)S(1)}, f32[6400,128,8]{1,0,2:T(8,128)}) fusion(pred[128,6400]{0,1:T(8,128)(4,1)S(1)} %fusion.40, bf16[1,128,1,8,128]{4,3,1,0,2:T(8,128)(2,1)S(1)} %constant_dynamic-slice_fusion.6, bf16[128,128]{1,0:T(8,128)(2,1)S(1)} %get-tuple-element.262, bf16[128,128]{1,0:T(8,128)(2,1)S(1)} %get-tuple-element.263, ...), kind=kOutput, calls=%fused_computation.10.clone.1 | convolution fusion | flops 1702296576 | bytes 28938240 | tf_op jit(solution)/shard_map/while/body/eval_jaxpr/tkgd,lkd->kgtl/dot_general | solution.py:22
  236.5 11.8 %fusion.42 = f32[8,128]{1,0:T(8,128)S(1)} fusion(f32[6400,128,8]{1,0,2:T(8,128)} %get-tuple-element.264, f32[8,128]{1,0:T(8,128)S(1)} %get-tuple-element.265, pred[128,6400]{0,1:T(8,128)(4,1)S(1)} %fusion.40), kind=kLoop, calls=%fused_computation.9.clone.1 | loop fusion | flops 26213376 | bytes 27041792 | tf_op jit(solution)/shard_map/while/body/eval_jaxpr/reduce_sum | solution.py:37
  248.5 1.7 copy.54
  250.2 0.1 copy.53
  250.3 12.7 %fusion.43 = bf16[128,8,128]{2,0,1:T(8,128)(2,1)S(1)} fusion(f32[8,128]{1,0:T(8,128)S(1)} %fusion.42, f32[8,128]{1,0:T(8,128)S(1)} %get-tuple-element.265, f32[6400,128,8]{1,0,2:T(8,128)} %get-tuple-element.264, pred[128,6400]{0,1:T(8,128)(4,1)S(1)} %fusion.40, bf16[128,128]{0,1:T(8,128)(2,1)S(1)} %bitcast.120, ...), kind=kOutput, calls=%fused_computation.28.clone.1 | convolution fusion | flops 1715535872 | bytes 28942336 | tf_op jit(solution)/shard_map/while/body/eval_jaxpr/kgtl,lkd->tkgd/dot_general | solution.py:38
  263.0 0.1 copy.55
  263.2 0.8 copy-done.8
  264.0 0.6 dynamic_slice.72
  264.6 0.6 iota_compare_fusion.7
  265.2 5.8 %fusion.40 = pred[128,6400]{0,1:T(8,128)(4,1)S(1)} fusion(s32[6400]{0:T(1024)S(1)} %iota_add_fusion.2, pred[6400]{0:T(1024)(128)(4,1)S(1)} %get-tuple-element.260, pred[6400]{0:T(1024)(128)(4,1)S(1)} %get-tuple-element.261), kind=kLoop, calls=%fused_computation.15.clone.1 | loop fusion | flops 2457600 | bytes 857600 | tf_op jit(solution)/shard_map/while/body/eval_jaxpr/or | solution.py:30
  271.0 1.5 dynamic-slice_bitcast_fusion.8
  272.5 13.3 %fusion.41 = (f32[8,128]{1,0:T(8,128)S(1)}, f32[6400,128,8]{1,0,2:T(8,128)}) fusion(pred[128,6400]{0,1:T(8,128)(4,1)S(1)} %fusion.40, bf16[1,128,1,8,128]{4,3,1,0,2:T(8,128)(2,1)S(1)} %constant_dynamic-slice_fusion.6, bf16[128,128]{1,0:T(8,128)(2,1)S(1)} %get-tuple-element.262, bf16[128,128]{1,0:T(8,128)(2,1)S(1)} %get-tuple-element.263, ...), kind=kOutput, calls=%fused_computation.10.clone.1 | convolution fusion | flops 1702296576 | bytes 28938240 | tf_op jit(solution)/shard_map/while/body/eval_jaxpr/tkgd,lkd->kgtl/dot_general | solution.py:22
  285.8 11.8 %fusion.42 = f32[8,128]{1,0:T(8,128)S(1)} fusion(f32[6400,128,8]{1,0,2:T(8,128)} %get-tuple-element.264, f32[8,128]{1,0:T(8,128)S(1)} %get-tuple-element.265, pred[128,6400]{0,1:T(8,128)(4,1)S(1)} %fusion.40), kind=kLoop, calls=%fused_computation.9.clone.1 | loop fusion | flops 26213376 | bytes 27041792 | tf_op jit(solution)/shard_map/while/body/eval_jaxpr/reduce_sum | solution.py:37
  297.7 1.7 copy.54
  299.4 0.1 copy.53
  299.5 12.3 %fusion.43 = bf16[128,8,128]{2,0,1:T(8,128)(2,1)S(1)} fusion(f32[8,128]{1,0:T(8,128)S(1)} %fusion.42, f32[8,128]{1,0:T(8,128)S(1)} %get-tuple-element.265, f32[6400,128,8]{1,0,2:T(8,128)} %get-tuple-element.264, pred[128,6400]{0,1:T(8,128)(4,1)S(1)} %fusion.40, bf16[128,128]{0,1:T(8,128)(2,1)S(1)} %bitcast.120, ...), kind=kOutput, calls=%fused_computation.28.clone.1 | convolution fusion | flops 1715535872 | bytes 28942336 | tf_op jit(solution)/shard_map/while/body/eval_jaxpr/kgtl,lkd->tkgd/dot_general | solution.py:38
  311.9 0.1 copy.55
  312.1 0.8 copy-done.8
  312.9 16.6 %all-gather.2.cloned.1.call-done = bf16[1024,8192]{1,0:T(8,128)(2,1)} async-done(((bf16[1024,2048]{1,0:T(8,128)(2,1)}), bf16[1024,8192]{1,0:T(8,128)(2,1)}) %all-gather.2.cloned.1.call-update) | async-done | bytes 16777232 | tf_op jit(solution)/shard_map/all_gather | solution.py:89
  329.5 12.5 %convolution_convert_fusion = bf16[256,8192]{1,0:T(8,128)(2,1)} fusion(bf16[256,1024]{1,0:T(8,128)(2,1)} %bitcast.129, bf16[1024,8192]{1,0:T(8,128)(2,1)} %all-gather.2.cloned.1.call-done), kind=kOutput, calls=%fused_computation.49 | convolution fusion | flops 4297064448 | bytes 21495808 | tf_op jit(solution)/shard_map/dot_general | solution.py:88
  342.0 92.8 %all-reduce.2.cloned.1.call-done = bf16[256,8192]{1,0:T(8,128)(2,1)} async-done(((bf16[256,8192]{1,0:T(8,128)(2,1)}), bf16[256,8192]{1,0:T(8,128)(2,1)}) %all-reduce.2.cloned.1.call-update) | async-done | bytes 4194320 | tf_op jit(solution)/shard_map/psum | solution.py:91
  434.9 4.6 %copy.66 = bf16[256,8192]{1,0:T(8,128)(2,1)} copy(bf16[256,8192]{1,0:T(8,128)(2,1)} %all-reduce.2.cloned.1.call-done) | data formatting | bytes 8388608
  (56 shorter events, 1.0 us)
Async XLA Ops:
  6.5 20.5 %copy-start = (bf16[64,128,128]{2,1,0:T(8,128)(2,1)S(1)}, bf16[64,128,128]{2,1,0:T(8,128)(2,1)}, u32[]{:S(2)}) copy-start(bf16[64,128,128]{2,1,0:T(8,128)(2,1)} %param.14) | copy-start | bytes 6291460
  35.1 5.0 %copy-start.3 = (bf16[64,128,128]{2,1,0:T(8,128)(2,1)S(1)}, bf16[64,128,128]{2,1,0:T(8,128)(2,1)}, u32[]{:S(2)}) copy-start(bf16[64,128,128]{2,1,0:T(8,128)(2,1)} %param.13) | copy-start | bytes 6291460
  35.1 82.9 %all-to-all-start.1 = ((bf16[192,128,128]{2,1,0:T(8,128)(2,1)}), bf16[192,128,128]{2,1,0:T(8,128)(2,1)}, u32[]{:S(2)}, u32[]{:S(2)}) async-start(bf16[192,128,128]{2,1,0:T(8,128)(2,1)} %gather_fusion.1), calls=%async_computation.1 | async-start | bytes 12582912 | tf_op jit(solution)/shard_map/all_to_all | solution.py:66
  118.0 91.1 %all-to-all-start.2 = ((bf16[192,128,128]{2,1,0:T(8,128)(2,1)}), bf16[192,128,128]{2,1,0:T(8,128)(2,1)}, u32[]{:S(2)}, u32[]{:S(2)}) async-start(bf16[192,128,128]{2,1,0:T(8,128)(2,1)} %gather_fusion.3), calls=%async_computation.2 | async-start | bytes 12582912 | tf_op jit(solution)/shard_map/all_to_all | solution.py:65
  122.9 0.8 copy-start.4
  122.9 3.0 copy-start.5
  123.0 6.9 %copy-start.6 = (bf16[256,1024]{1,0:T(8,128)(2,1)S(1)}, bf16[256,1024]{1,0:T(8,128)(2,1)}, u32[]{:S(2)}) copy-start(bf16[256,1024]{1,0:T(8,128)(2,1)} %param.10) | copy-start | bytes 1572868
  123.0 206.6 %all-gather.2.cloned.1.call-start = ((), (), s32[]{:S(2)}) async-start(), calls=%async_computation.3 | async-start | bytes 20971520 | tf_op jit(solution)/shard_map/all_gather | solution.py:89
  123.7 311.1 %all-reduce.2.cloned.1.call-start = ((), (), s32[]{:S(2)}) async-start(), calls=%async_computation.4 | async-start | bytes 8388608 | tf_op jit(solution)/shard_map/psum | solution.py:91
  123.9 6.0 %collective-permute-start = (bf16[128,128]{0,1:T(8,128)(2,1)S(1)}, bf16[128,128]{0,1:T(8,128)(2,1)S(1)}, u32[]{:S(2)}, u32[]{:S(2)}) collective-permute-start(bf16[128,128]{0,1:T(8,128)(2,1)S(1)} %copy.41), channel_id=1, source_target_pairs={{0,4},{4,8},{8,12},{12,16},{16,20},{20,24},{24,28},{28,32},{32,36}... | collective-permute-start | bytes 98312 | tf_op jit(solution)/shard_map/ppermute | solution.py:12
  125.9 4.4 collective-permute-start.1
  236.5 11.9 %copy-start.2 = (bf16[2,6144,128]{2,1,0:T(8,128)(2,1)S(1)}, bf16[2,6144,128]{2,1,0:T(8,128)(2,1)}, u32[]{:S(2)}) copy-start(bf16[2,6144,128]{2,1,0:T(8,128)(2,1)} %get-tuple-element.290) | copy-start | bytes 9437188 | tf_op jit(solution)/shard_map/while
  250.3 12.9 %copy-start.7 = (bf16[2,128,1024]{2,1,0:T(8,128)(2,1)S(1)}, bf16[2,128,1024]{2,1,0:T(8,128)(2,1)}, u32[]{:S(2)}) copy-start(bf16[2,128,1024]{2,1,0:T(8,128)(2,1)} %get-tuple-element.278) | copy-start | bytes 1572868 | tf_op jit(solution)/shard_map/while
  263.2 0.8 copy-start.8
  285.8 11.8 %copy-start.2 = (bf16[2,6144,128]{2,1,0:T(8,128)(2,1)S(1)}, bf16[2,6144,128]{2,1,0:T(8,128)(2,1)}, u32[]{:S(2)}) copy-start(bf16[2,6144,128]{2,1,0:T(8,128)(2,1)} %get-tuple-element.290) | copy-start | bytes 9437188 | tf_op jit(solution)/shard_map/while
  299.5 12.5 %copy-start.7 = (bf16[2,128,1024]{2,1,0:T(8,128)(2,1)S(1)}, bf16[2,128,1024]{2,1,0:T(8,128)(2,1)}, u32[]{:S(2)}) copy-start(bf16[2,128,1024]{2,1,0:T(8,128)(2,1)} %get-tuple-element.278) | copy-start | bytes 1572868 | tf_op jit(solution)/shard_map/while
  312.1 0.8 copy-start.8
  342.0 97.5 %copy-start.1 = (bf16[64,128,128]{2,1,0:T(8,128)(2,1)S(1)}, bf16[64,128,128]{2,1,0:T(8,128)(2,1)}, u32[]{:S(2)}) copy-start(bf16[64,128,128]{2,1,0:T(8,128)(2,1)} %param.14) | copy-start | bytes 6291460
Sparse Core Ops, SparseCore 0:
  125.4 204.0 all-gather.1
  342.1 92.6 all-reduce.1
where the time goes:
time: 448 us; the launch traced here: 446 us
  waiting for transfers between devices  254 us (57%)
  matrix products  64.1 us (14%)
  local copies, waits for them, and re-layouts  46.1 us (10%)
  other arithmetic  37.3 us (8%)
  starting transfers between devices  15.7 us (4%)
  blocking collectives  15.5 us (3%)
  between operations  13.6 us (3%)
    psum x1, waiting for transfers between devices, body(): mixed = lax.psum(partial_terms.astype(jnp.bfloat16), 'head')  92.8 us
    all_to_all x1, waiting for transfers between devices, body(): lax.all_to_all(send_k, ('fsdp', 'seq'), split_axis=0, concat_axis=0, tile...  73.3 us
    all_to_all x1, waiting for transfers between devices, body(): lax.all_to_all(send_v, ('fsdp', 'seq'), split_axis=0, concat_axis=0, tile...  69.9 us
    dot_general x2, matrix products, attend_block(): jnp.einsum('tkgd,lkd->kgtl', query_block, keys_four, preferred_element_ty...  26.6 us
    dot_general x2, matrix products, attend_block(): jnp.einsum('kgtl,lkd->tkgd', probs_bf, values_four, preferred_element_typ...  25 us
    reduce_sum x2, other arithmetic, attend_block(): jnp.sum(expo, axis=-1, keepdims=True)  23.7 us
    all_gather x1, waiting for transfers between devices, body(): lax.all_gather(wo, 'fsdp', axis=1, tiled=True)  16.6 us
    all_to_all x1, blocking collectives, body(): lax.all_to_all(wanted.reshape(seq_devs, capacity), ('fsdp', 'seq'), split...  15.5 us
  transfers between devices with their start and end apart: 6, of which 5 were waited for; matrix products, arithmetic and copies ran while one was open for 26% of the time, Pallas kernels for 0%

commit v1 on v0

v1 whole, which is shorter than its diff:
```python
import functools

import jax
import jax.numpy as jnp
from jax import lax
from jax.experimental import pallas as pl
from jax.experimental.pallas import tpu as pltpu
from jax.sharding import PartitionSpec as P

HD = 128
BLK = 128
NEG = -1e30
MESH = pl.DeviceIdType.MESH
BF16 = jnp.bfloat16
F32 = jnp.float32
LOG2E = 1.4426950408889634


def position():
    z = lax.axis_index("fsdp")
    s = lax.axis_index("seq")
    y = lax.axis_index("head")
    return z, s // 2, s % 2, y


def dev(z, x, c, y):
    return ((z + 4) % 4, ((x + 4) % 4) * 2 + c, (y + 4) % 4)


def gather_kernel(q_ref, ck_ref, cv_ref, sk_ref, sv_ref, tab_ref,
                  qall_ref, pk_ref, pv_ref, prev_ref, taball_ref,
                  send_sem, recv_sem, loc_sem):
    z, x, c, y = position()
    far_z, far_x = (z, x + jnp.where(c == 0, -1, 1))
    wrap = jnp.where(c == 0, jnp.where(x == 0, -1, 0), jnp.where(x == 3, 1, 0))
    far_z = far_z + wrap

    barrier = pltpu.get_barrier_semaphore()
    for off in range(1, 16):
        pl.semaphore_signal(barrier, inc=1, device_id=dev(z + off // 4, x + off % 4, c, y), device_id_type=MESH)
    pl.semaphore_signal(barrier, inc=1, device_id=dev(z, x, 1 - c, y), device_id_type=MESH)
    pl.semaphore_signal(barrier, inc=1, device_id=dev(far_z, far_x, 1 - c, y), device_id_type=MESH)
    pl.semaphore_wait(barrier, 17)

    copies = []

    def send(src, dst, target):
        k = len(copies)
        cp = pltpu.make_async_remote_copy(
            src_ref=src, dst_ref=dst, send_sem=send_sem.at[k], recv_sem=recv_sem.at[k],
            device_id=target, device_id_type=MESH)
        cp.start()
        copies.append(cp)
        return cp

    def slot(dz, dx):
        return ((z + dz + 4) % 4) * 4 + (x + dx + 4) % 4

    here = slot(0, 0)
    tables = []
    for off in range(1, 16):
        dz, dx = off // 4, off % 4
        tables.append(send(tab_ref.at[slot(dz, dx)], taball_ref.at[here], dev(z + dz, x + dx, c, y)))
    nxt_x = x + jnp.where(c == 0, 0, 1)
    nxt_z = z + jnp.where((c == 1) & (x == 3), 1, 0)
    nxt = dev(nxt_z, nxt_x, 1 - c, y)
    send(sk_ref.at[pl.ds(BLK, BLK)], prev_ref.at[0], nxt)
    send(sv_ref.at[pl.ds(BLK, BLK)], prev_ref.at[1], nxt)

    def step(color, major, minor):
        return (minor, major) if color == 0 else (major, minor)

    def chunk(color, a, b, half=None):
        dz, dx = step(color, a, b)
        ref = qall_ref.at[slot(dz, dx), color]
        if half is None:
            return ref
        return ref.at[pl.ds(half * (BLK // 2), BLK // 2)]

    def to(color, a, b):
        dz, dx = step(color, a, b)
        return dev(z + dz, x + dx, c, y)

    ring = {}

    def own(color):
        mine, dst = q_ref.at[color], qall_ref.at[here, color]
        for d in (1, -1):
            ring[color, "a", d] = send(mine, dst, to(color, d, 0))
        for d in (1, -1):
            ring[color, "b", 0, d] = send(mine, dst, to(color, 0, d))

    own(0)
    own(1)
    partner = dev(z, x, 1 - c, y)
    send(ck_ref, pk_ref, partner)
    send(cv_ref, pv_ref, partner)
    locals_ = [pltpu.make_async_copy(q_ref, qall_ref.at[here], loc_sem.at[0]),
               pltpu.make_async_copy(tab_ref.at[here], taball_ref.at[here], loc_sem.at[1])]
    for cp in locals_:
        cp.start()

    for d in (1, -1):
        for color in (0, 1):
            ring[color, "a", d].wait_recv()
            half = 0 if d == 1 else 1
            part = chunk(color, -d, 0, half)
            ring[color, "o", d] = send(part, part, to(color, d, 0))
            whole = chunk(color, -d, 0)
            for e in (1, -1):
                ring[color, "b", -d, e] = send(whole, whole, to(color, 0, e))
    for d in (1, -1):
        for color in (0, 1):
            ring[color, "b", 0, d].wait_recv()
            part = chunk(color, 0, -d, 0 if d == 1 else 1)
            ring[color, "c", 0, d] = send(part, part, to(color, 0, d))
    for color in (0, 1):
        ring[color, "o", 1].wait_recv()
        ring[color, "o", -1].wait_recv()
        whole = chunk(color, 2, 0)
        for e in (1, -1):
            ring[color, "b", 2, e] = send(whole, whole, to(color, 0, e))
    for a in (-1, 1, 2):
        for d in (1, -1):
            for color in (0, 1):
                ring[color, "b", a, d].wait_recv()
                part = chunk(color, a, -d, 0 if d == 1 else 1)
                ring[color, "c", a, d] = send(part, part, to(color, 0, d))
    waited = {id(v) for k, v in ring.items() if k[1] != "c"}
    for cp in copies:
        if id(cp) not in waited:
            cp.wait_recv()
    for cp in copies:
        cp.wait_send()
    for cp in locals_:
        cp.wait()


N_GATHER = 15 + 2 + 8 + 2 + 4 + 8 + 4 + 4 + 12


def gather_queries(q, ck, cv, sk, sv, tab):
    anyspec = pl.BlockSpec(memory_space=pl.ANY)
    return pl.pallas_call(
        gather_kernel,
        out_shape=(
            jax.ShapeDtypeStruct((16, 2, BLK, q.shape[-1]), BF16),
            jax.ShapeDtypeStruct(ck.shape, BF16),
            jax.ShapeDtypeStruct(cv.shape, BF16),
            jax.ShapeDtypeStruct((2, BLK, HD), BF16),
            jax.ShapeDtypeStruct(tab.shape, jnp.int32),
        ),
        in_specs=[anyspec] * 6,
        out_specs=[anyspec] * 5,
        scratch_shapes=[
            pltpu.SemaphoreType.DMA((N_GATHER,)),
            pltpu.SemaphoreType.DMA((N_GATHER,)),
            pltpu.SemaphoreType.DMA((2,)),
        ],
        compiler_params=pltpu.CompilerParams(collective_id=0, has_side_effects=True),
        name="gather_queries",
    )(q, ck, cv, sk, sv, tab)


def attend_kernel(tab_ref, q_ref, ck_ref, cv_ref, pk_ref, pv_ref, sk_ref, sv_ref, prev_ref, out_ref,
                  kall, vall, span, qt, m_s, l_s, acc, sems):
    i = pl.program_id(0)
    z, x, c, y = position()
    chip = i // 2
    color = i % 2
    mine = chip == z * 4 + x

    @pl.when(i == 0)
    def _():
        loads = [
            pltpu.make_async_copy(ck_ref, kall.at[pl.ds(0, 64)], sems.at[0]),
            pltpu.make_async_copy(pk_ref, kall.at[pl.ds(64, 64)], sems.at[1]),
            pltpu.make_async_copy(cv_ref, vall.at[pl.ds(0, 64)], sems.at[2]),
            pltpu.make_async_copy(pv_ref, vall.at[pl.ds(64, 64)], sems.at[3]),
            pltpu.make_async_copy(prev_ref.at[0], span.at[0, pl.ds(0, BLK)], sems.at[4]),
            pltpu.make_async_copy(prev_ref.at[1], span.at[1, pl.ds(0, BLK)], sems.at[5]),
            pltpu.make_async_copy(sk_ref, span.at[0, pl.ds(BLK, 2 * BLK)], sems.at[6]),
            pltpu.make_async_copy(sv_ref, span.at[1, pl.ds(BLK, 2 * BLK)], sems.at[7]),
        ]
        for cp in loads:
            cp.start()
        for cp in loads:
            cp.wait()

    heads = q_ref.shape[-1] // HD
    for g in range(heads):
        qt[:, g * HD:(g + 1) * HD] = q_ref[0, 0, :, g * HD:(g + 1) * HD].T
    m_s[...] = jnp.full_like(m_s, NEG)
    l_s[...] = jnp.zeros_like(l_s)
    acc[...] = jnp.zeros_like(acc)
    scale = LOG2E / (HD ** 0.5)
    width = 256

    def pair(keys, values, bias):
        for t in range(heads * HD // width):
            cols = slice(t * width, (t + 1) * width)
            s = jnp.dot(keys, qt[:, cols], preferred_element_type=F32) * scale
            if bias is not None:
                s = s + bias
            top = jnp.maximum(m_s[:, cols], jnp.max(s, axis=0, keepdims=True))
            old = jnp.exp2(m_s[:, cols] - top)
            p = jnp.exp2(s - top)
            m_s[:, cols] = top
            l_s[:, cols] = l_s[:, cols] * old + jnp.sum(p, axis=0, keepdims=True)
            acc[:, cols] = acc[:, cols] * old + lax.dot_general(
                values, p.astype(BF16), (((0,), (0,)), ((), ())), preferred_element_type=F32)

    count = tab_ref[chip, 0, color * 16 + 15]
    base = color * 16

    def both(j, carry):
        i0 = tab_ref[chip, 0, base + 2 * j]
        i1 = tab_ref[chip, 0, base + 2 * j + 1]
        keys = jnp.concatenate([kall[i0], kall[i1]], axis=0)
        values = jnp.concatenate([vall[i0], vall[i1]], axis=0)
        pair(keys, values, None)
        return carry

    lax.fori_loop(0, count // 2, both, 0)

    @pl.when(count % 2 == 1)
    def _():
        i0 = tab_ref[chip, 0, base + count - 1]
        pair(kall[i0], vall[i0], None)

    @pl.when(mine)
    def _():
        rows = pl.ds(pl.multiple_of(color * BLK, BLK), 2 * BLK)
        key = lax.broadcasted_iota(jnp.int32, (2 * BLK, width), 0)
        tok = lax.broadcasted_iota(jnp.int32, (2 * BLK, width), 1) % BLK
        first = (z * 8 + x * 2 + c) * 2 + color == 0
        low = jnp.where(first, BLK, 0)
        allowed = (key >= low) & (key - BLK <= tok)
        pair(span[0, rows, :], span[1, rows, :], jnp.where(allowed, 0.0, 2 * NEG))

    some = l_s[...] > 0
    total = jnp.where(some, l_s[...], 1.0)
    lse = m_s[...] + jnp.log2(total)
    hi = lse.astype(BF16)
    rest = lse - hi.astype(F32)
    mid = rest.astype(BF16)
    low_ = (rest - mid.astype(F32)).astype(BF16)
    o = (acc[...] / total).astype(BF16)
    row = lax.broadcasted_iota(jnp.int32, (16, lse.shape[1]), 0)
    tail = jnp.where(row == 0, hi.astype(F32), jnp.where(row == 1, mid.astype(F32), jnp.where(row == 2, low_.astype(F32), 0.0))).astype(BF16)
    half = lse.shape[1] // 2
    for h in range(2):
        out_ref[0, 0, h, 0:HD, :] = o[:, h * half:(h + 1) * half]
        out_ref[0, 0, h, HD:HD + 16, :] = tail[:, h * half:(h + 1) * half]


def attend(tab, q_all, ck, cv, pk, pv, sk, sv, prev):
    width = q_all.shape[-1]
    anyspec = pl.BlockSpec(memory_space=pl.ANY)
    return pl.pallas_call(
        attend_kernel,
        out_shape=jax.ShapeDtypeStruct((16, 2, 2, HD + 16, width // 2), BF16),
        grid_spec=pltpu.PrefetchScalarGridSpec(
            num_scalar_prefetch=1,
            grid=(32,),
            in_specs=[pl.BlockSpec((1, 1, BLK, width), lambda i, t: (i // 2, i % 2, 0, 0))] + [anyspec] * 7,
            out_specs=pl.BlockSpec((1, 1, 2, HD + 16, width // 2), lambda i, t: (i // 2, i % 2, 0, 0, 0)),
            scratch_shapes=[
                pltpu.VMEM((128, BLK, HD), BF16),
                pltpu.VMEM((128, BLK, HD), BF16),
                pltpu.VMEM((2, 3 * BLK, HD), BF16),
                pltpu.VMEM((HD, width), BF16),
                pltpu.VMEM((1, width), F32),
                pltpu.VMEM((1, width), F32),
                pltpu.VMEM((HD, width), F32),
                pltpu.SemaphoreType.DMA((8,)),
            ],
        ),
        compiler_params=pltpu.CompilerParams(vmem_limit_bytes=40 * 2**20),
        cost_estimate=pl.CostEstimate(flops=7_000_000_000, bytes_accessed=26_000_000, transcendentals=13_000_000),
        name="attend",
    )(tab, q_all, ck, cv, pk, pv, sk, sv, prev)


def merge(dst, *srcs):
    def lse_of(ref):
        t = ref[HD:HD + 16, :].astype(F32)
        return t[0:1] + t[1:2] + t[2:3]

    lses = [lse_of(r) for r in srcs]
    top = functools.reduce(jnp.maximum, lses)
    ws = [jnp.exp2(v - top) for v in lses]
    total = functools.reduce(lambda a, b: a + b, ws)
    inv = 1.0 / total
    ws = [w * inv for w in ws]
    lse = top + jnp.log2(total)
    rows = 32

    def body(r, carry):
        sl = pl.ds(pl.multiple_of(r * rows, rows), rows)
        out = ws[0] * srcs[0][sl, :].astype(F32)
        for w, ref in zip(ws[1:], srcs[1:]):
            out = out + w * ref[sl, :].astype(F32)
        dst[sl, :] = out.astype(BF16)
        return carry

    lax.fori_loop(0, HD // rows, body, 0)
    hi = lse.astype(BF16).astype(F32)
    mid = (lse - hi).astype(BF16).astype(F32)
    low = lse - hi - mid
    row = lax.broadcasted_iota(jnp.int32, (16, lse.shape[1]), 0)
    dst[HD:HD + 16, :] = jnp.where(row == 0, hi, jnp.where(row == 1, mid, jnp.where(row == 2, low, 0.0))).astype(BF16)


def reduce_kernel(part_ref, out_ref, loc, recv, send_sem, recv_sem, load_sem):
    z, x, c, y = position()
    barrier = pltpu.get_barrier_semaphore()
    for dz, dx in ((0, 1), (0, -1), (1, 0), (-1, 0)):
        pl.semaphore_signal(barrier, inc=1, device_id=dev(z + dz, x + dx, c, y), device_id_type=MESH)

    def step(color, a, b):
        return (a, b) if color == 0 else (b, a)

    def slot(color, a, b):
        dz, dx = step(color, a, b)
        return ((z + dz + 4) % 4) * 4 + (x + dx + 4) % 4

    def to(color, a, b):
        dz, dx = step(color, a, b)
        return dev(z + dz, x + dx, c, y)

    order = [2, 1, 3, 0]
    loads = {}
    k = 0
    for a in (2, 1, 3, 0):
        for b in order:
            for color in (0, 1):
                cp = pltpu.make_async_copy(
                    part_ref.at[slot(color, a, b), color], loc.at[color, a * 4 + b], load_sem.at[k])
                cp.start()
                loads[color, a, b] = cp
                k += 1
    pl.semaphore_wait(barrier, 4)

    copies = {}

    def send(key, src, target):
        k = len(copies)
        cp = pltpu.make_async_remote_copy(
            src_ref=src, dst_ref=recv.at[k], send_sem=send_sem.at[k], recv_sem=recv_sem.at[k],
            device_id=target, device_id_type=MESH)
        cp.start()
        copies[key] = (cp, k)

    def got(key):
        cp, k = copies[key]
        cp.wait_recv()
        return recv.at[k]

    def piece(color, a, b, half):
        return loc.at[color, a * 4 + b, half]

    for b in order:
        for color in (0, 1):
            loads[color, 2, b].wait()
            send((color, 1, b, "op"), piece(color, 2, b, 0), to(color, 1, 0))
            send((color, 1, b, "om"), piece(color, 2, b, 1), to(color, -1, 0))
    for b in order:
        for color in (0, 1):
            loads[color, 1, b].wait()
            send((color, 1, b, "p1"), piece(color, 1, b, 1), to(color, 1, 0))
            loads[color, 3, b].wait()
            send((color, 1, b, "m0"), piece(color, 3, b, 0), to(color, -1, 0))
    for b in order:
        for color in (0, 1):
            r = got((color, 1, b, "op"))
            merge(piece(color, 1, b, 0), piece(color, 1, b, 0), r)
            send((color, 1, b, "p0"), piece(color, 1, b, 0), to(color, 1, 0))
            r = got((color, 1, b, "om"))
            merge(piece(color, 3, b, 1), piece(color, 3, b, 1), r)
            send((color, 1, b, "m1"), piece(color, 3, b, 1), to(color, -1, 0))
    for b in order:
        for color in (0, 1):
            loads[color, 0, b].wait()
            for half in (0, 1):
                p = got((color, 1, b, "p%d" % half))
                m = got((color, 1, b, "m%d" % half))
                merge(piece(color, 0, b, half), piece(color, 0, b, half), p, m)
            if b == 2:
                send((color, 2, "op"), piece(color, 0, 2, 0), to(color, 0, 1))
                send((color, 2, "om"), piece(color, 0, 2, 1), to(color, 0, -1))
            if b == 1:
                send((color, 2, "p1"), piece(color, 0, 1, 1), to(color, 0, 1))
            if b == 3:
                send((color, 2, "m0"), piece(color, 0, 3, 0), to(color, 0, -1))
    for color in (0, 1):
        r = got((color, 2, "op"))
        merge(piece(color, 0, 1, 0), piece(color, 0, 1, 0), r)
        send((color, 2, "p0"), piece(color, 0, 1, 0), to(color, 0, 1))
        r = got((color, 2, "om"))
        merge(piece(color, 0, 3, 1), piece(color, 0, 3, 1), r)
        send((color, 2, "m1"), piece(color, 0, 3, 1), to(color, 0, -1))
    for color in (0, 1):
        for half in (0, 1):
            p = got((color, 2, "p%d" % half))
            m = got((color, 2, "m%d" % half))
            own = piece(color, 0, 0, half)
            merge(own, own, p, m)
            lanes = own.shape[1]
            for g in range(lanes // HD):
                col = half * lanes + g * HD
                out_ref[color * BLK:(color + 1) * BLK, col:col + HD] = own[0:HD, g * HD:(g + 1) * HD].T
    for cp, _ in copies.values():
        cp.wait_send()


N_REDUCE = 60


def reduce_partials(part):
    rows, lanes = part.shape[-2:]
    return pl.pallas_call(
        reduce_kernel,
        out_shape=jax.ShapeDtypeStruct((2 * BLK, 2 * lanes), BF16),
        in_specs=[pl.BlockSpec(memory_space=pl.ANY)],
        out_specs=pl.BlockSpec(memory_space=pltpu.VMEM),
        scratch_shapes=[
            pltpu.VMEM((2, 16, 2, rows, lanes), BF16),
            pltpu.VMEM((N_REDUCE, rows, lanes), BF16),
            pltpu.SemaphoreType.DMA((N_REDUCE,)),
            pltpu.SemaphoreType.DMA((N_REDUCE,)),
            pltpu.SemaphoreType.DMA((32,)),
        ],
        compiler_params=pltpu.CompilerParams(
            collective_id=1, has_side_effects=True, vmem_limit_bytes=40 * 2**20),
        name="reduce_partials",
    )(part)


def request_table(block_slot, pattern, core, cb_local):
    slot_ids = block_slot[pattern]
    owners = slot_ids // cb_local
    chips = owners // 2
    rel = jnp.where(owners % 2 == core, 0, cb_local) + slot_ids % cb_local
    entry = jnp.arange(pattern.shape[1])
    same = (chips[:, :, None] == chips[:, None, :]) & (entry[None, :] < entry[:, None])[None]
    rank = jnp.sum(same.astype(jnp.int32), axis=2)
    lane = jnp.arange(16)
    hit = (chips[None, :, None, :] == jnp.arange(16)[:, None, None, None])
    pick = hit & (rank[None, :, None, :] == lane[None, None, :, None])
    value = jnp.where(lane[None, None, :, None] == 15, hit.astype(jnp.int32), jnp.where(pick, rel[None, :, None, :], 0))
    table = jnp.sum(value, axis=3).reshape(16, 1, 32)
    return jnp.pad(table, ((0, 0), (0, 0), (0, 96)))


def body(queries, span_k, span_v, cache_k, cache_v, block_slot, pattern, wo):
    core = lax.axis_index("seq") % 2
    tab = request_table(block_slot, pattern, core, cache_k.shape[0])
    q = queries.reshape(2, BLK, queries.shape[1])
    q_all, pk, pv, prev, tab_all = gather_queries(q, cache_k, cache_v, span_k, span_v, tab)
    part = attend(tab_all, q_all, cache_k, cache_v, pk, pv, span_k, span_v, prev)
    attended = reduce_partials(part)
    partial_terms = jnp.dot(
        attended, lax.all_gather(wo, "fsdp", axis=1, tiled=True), preferred_element_type=F32
    )
    return lax.psum(partial_terms.astype(BF16), "head")


def solution(mesh):
    return jax.shard_map(
        body,
        mesh=mesh,
        in_specs=(
            P(("fsdp", "seq"), "head"),
            P(("fsdp", "seq"), "head"),
            P(("fsdp", "seq"), "head"),
            P(("fsdp", "seq"), None, "head"),
            P(("fsdp", "seq"), None, "head"),
            P(),
            P(("fsdp", "seq"), None),
            P("head", "fsdp"),
        ),
        out_specs=P(("fsdp", "seq"), None),
        check_vma=False,
    )
```

time: 448 us -> 361 us (0.81)
  Pallas kernels: 0 us -> 225 us
  waiting for transfers between devices: 254 us -> 92.3 us
  matrix products: 64.1 us -> 11.9 us
  other arithmetic: 37.3 us -> 0.98 us
  local copies, waits for them, and re-layouts: 46.1 us -> 16.8 us
  starting transfers between devices: 15.7 us -> 0.08 us
  blocking collectives: 15.5 us -> 0 us
    pallas_call x0 -> x3, Pallas kernels: none -> 225 us  [the longest x1 85.7 us: gather_queries(): pl.pallas_call(gather_kernel, out_shape=(jax.ShapeDtypeStruct((16, 2, BLK...]
    all_to_all x2 -> x0, waiting for transfers between devices: 143 us -> none  [the longest x1 73.3 us: body(): lax.all_to_all(send_k, ('fsdp', 'seq'), split_axis=0, concat_axis=0, tile...]
    dot_general x4 -> x0, matrix products: 51.7 us -> none  [the longest x2 26.6 us: attend_block(): jnp.einsum('tkgd,lkd->kgtl', query_block, keys_four, preferred_element_ty...]
    gather x5 -> x2, local copies, waits for them, and re-layouts: 28.6 us -> 1.23 us  [request_table(): slot_ids = block_slot[pattern]]
    reduce_sum x3 -> x2, other arithmetic: 23.8 us -> 0.9 us  [the longest x1 0.72 us: request_table(): table = jnp.sum(value, axis=3).reshape(16, 1, 32)]
    all_gather x1, waiting for transfers between devices: 16.6 us -> 0.02 us  [body(): lax.all_gather(wo, 'fsdp', axis=1, tiled=True)]
    all_to_all x1 -> x0, blocking collectives: 15.5 us -> none  [body(): lax.all_to_all(wanted.reshape(seq_devs, capacity), ('fsdp', 'seq'), split...]
    or x2 -> x0, other arithmetic: 11.5 us -> none  [attend_block(): (column < listed_end) | (column >= listed_end) & (column < own_start) & p...]
  transfers between devices with their start and end apart: 6 -> 2, of which waited for: 5 -> 1; matrix products, arithmetic and copies ran while one was open for 26% -> 1% of each run, Pallas kernels for 0% -> 62%
where the time goes in v1:
time: 361 us; the launch traced here: 360 us
  Pallas kernels  225 us (62%)
  waiting for transfers between devices  92.3 us (26%)
  local copies, waits for them, and re-layouts  16.8 us (5%)
  between operations  13.6 us (4%)
  matrix products  11.9 us (3%)
    psum x1, waiting for transfers between devices, body(): return lax.psum(partial_terms.astype(BF16), 'head')  91.6 us
    pallas_call x1, Pallas kernels, gather_queries(): pl.pallas_call(gather_kernel, out_shape=(jax.ShapeDtypeStruct((16, 2, BLK...  85.7 us
    pallas_call x1, Pallas kernels, attend(): pl.pallas_call(attend_kernel, out_shape=jax.ShapeDtypeStruct((16, 2, 2, H...  74 us
    pallas_call x1, Pallas kernels, reduce_partials(): pl.pallas_call(reduce_kernel, out_shape=jax.ShapeDtypeStruct((2 * BLK, 2...  65 us
    unnamed x23, local copies, waits for them, and re-layouts  14.8 us
    dot_general x1, matrix products, body(): jnp.dot(attended, lax.all_gather(wo, 'fsdp', axis=1, tiled=True), preferr...  11.9 us
  transfers between devices with their start and end apart: 2, of which 1 were waited for; matrix products, arithmetic and copies ran while one was open for 1% of the time, Pallas kernels for 62%

profile of v1, /device:TPU:0, one launch (start us, length us, event | category | flops | bytes accessed | tf_op | source)
XLA Modules:
  0.0 360.2 jit_solution(9717275844101904301)
XLA Ops:
  6.5 0.0 copy-start
  6.5 0.0 copy-start.10
  6.5 0.0 copy-start.7
  6.5 0.0 copy-start.2
  6.5 0.0 copy-start.6
  6.6 0.0 all-gather.2.cloned.1.call-start
  6.6 0.7 all-gather.2.cloned.1.call-update
  7.3 0.0 all-reduce.3.cloned.1.call-start
  7.3 0.0 copy-done.10
  7.4 0.1 reshape.168
  7.5 0.0 copy-done
  7.5 1.1 gather_fusion
  8.6 0.1 reshape.167
  8.7 0.2 convert_reduce_fusion
  9.0 0.7 select_reduce_fusion
  9.7 0.1 reshape.165
  9.8 0.6 pad.4.tab_ref
  10.4 85.7 %gather_queries.1 = (bf16[16,2,128,1024]{3,2,1,0:T(8,128)(2,1)}, bf16[64,128,128]{2,1,0:T(8,128)(2,1)}, bf16[64,128,128]{2,1,0:T(8,128)(2,1)}, bf16[2,128,128]{2,1,0:T(8,128)(2,1)}, s32[16,1,128]{2,1,0:T(1,128)}) custom-call(bf16[2,128,1024]{2,1,0:T(8,128)(2,1)} %bitcast.3, bf16[64,128,128]{2,1,0:T(8,128)(2,1)} %ck_ref.3, bf16[64,128,128]{2,1,0:T(8,128)(2,1)} %cv_ref.3, ...), custom_call_target="tpu_custom_call" | custom-call | tf_op jit(solution)/shard_map/gather_queries/pallas_call | solution.py:144
  96.1 0.0 copy-done.7
  96.1 0.0 copy-done.2
  96.1 0.0 copy-done.6
  96.1 0.0 copy-start.3
  96.1 1.6 copy-done.3
  97.8 0.0 copy-start.4
  97.8 1.6 copy-done.4
  99.4 0.0 copy-start.5
  99.4 1.6 copy-done.5
  101.0 0.0 copy-start.8
  101.0 0.8 copy-done.8
  101.9 0.0 copy-start.9
  101.9 0.7 copy-done.9
  102.6 74.0 %attend.1.part_ref = bf16[16,2,2,144,512]{4,3,2,1,0:T(8,128)(2,1)} custom-call(s32[16,1,128]{2,1,0:T(1,128)S(1)} %copy-done.9, bf16[16,2,128,1024]{3,2,1,0:T(8,128)(2,1)} %get-tuple-element.11.q_ref, bf16[64,128,128]{2,1,0:T(8,128)(2,1)S(1)} %copy-done.2, bf16[64,128,128]{2,1,0:T(8,128)(2,1)S(1)} %copy-done.3, bf16[64,128,128]{2,1,0:T(8,128)(2,1)S(1)} %copy-done.4, ...), custom_call_target="tpu_custom_call" | custom-call | flops 7000000000 | bytes 26000000 | tf_op jit(solution)/shard_map/attend/pallas_call | solution.py:260
  176.6 0.0 copy-start.1
  176.6 3.7 %copy-done.1 = bf16[16,2,2,144,512]{4,3,2,1,0:T(8,128)(2,1)S(1)} copy-done((bf16[16,2,2,144,512]{4,3,2,1,0:T(8,128)(2,1)S(1)}, bf16[16,2,2,144,512]{4,3,2,1,0:T(8,128)(2,1)}, u32[]{:S(2)}) %copy-start.1) | copy-done | bytes 9437208
  180.3 65.0 %reduce_partials.1 = bf16[256,1024]{1,0:T(8,128)(2,1)S(1)} custom-call(bf16[16,2,2,144,512]{4,3,2,1,0:T(8,128)(2,1)S(1)} %copy-done.1), custom_call_target="tpu_custom_call" | custom-call | tf_op jit(solution)/shard_map/reduce_partials/pallas_call | solution.py:422
  245.3 0.0 all-gather.2.cloned.1.call-done
  245.3 11.9 %convolution_convert_fusion = bf16[256,8192]{1,0:T(8,128)(2,1)} fusion(bf16[256,1024]{1,0:T(8,128)(2,1)S(1)} %reduce_partials.1, bf16[1024,8192]{1,0:T(8,128)(2,1)} %all-gather.2.cloned.1.call-done), kind=kOutput, calls=%fused_computation.1 | convolution fusion | flops 4297064448 | bytes 21495808 | tf_op jit(solution)/shard_map/dot_general | solution.py:463
  257.2 0.0 all-reduce.3.cloned.1.call-update
  257.2 91.6 %all-reduce.3.cloned.1.call-done = bf16[256,8192]{1,0:T(8,128)(2,1)} async-done(((bf16[256,8192]{1,0:T(8,128)(2,1)}), bf16[256,8192]{1,0:T(8,128)(2,1)}) %all-reduce.3.cloned.1.call-update) | async-done | bytes 4194320 | tf_op jit(solution)/shard_map/psum | solution.py:466
  348.8 4.6 %copy.10 = bf16[256,8192]{1,0:T(8,128)(2,1)} copy(bf16[256,8192]{1,0:T(8,128)(2,1)} %all-reduce.3.cloned.1.call-done) | data formatting | bytes 8388608
  (8 shorter events, 0.1 us)
Async XLA Ops:
  6.5 0.9 copy-start
  6.5 0.8 copy-start.10
  6.5 89.6 %copy-start.7 = (bf16[256,128]{1,0:T(8,128)(2,1)S(1)}, bf16[256,128]{1,0:T(8,128)(2,1)}, u32[]{:S(2)}) copy-start(bf16[256,128]{1,0:T(8,128)(2,1)} %sv_ref.3) | copy-start | bytes 196612
  6.5 89.6 %copy-start.2 = (bf16[64,128,128]{2,1,0:T(8,128)(2,1)S(1)}, bf16[64,128,128]{2,1,0:T(8,128)(2,1)}, u32[]{:S(2)}) copy-start(bf16[64,128,128]{2,1,0:T(8,128)(2,1)} %ck_ref.3) | copy-start | bytes 6291460
  6.5 89.6 %copy-start.6 = (bf16[256,128]{1,0:T(8,128)(2,1)S(1)}, bf16[256,128]{1,0:T(8,128)(2,1)}, u32[]{:S(2)}) copy-start(bf16[256,128]{1,0:T(8,128)(2,1)} %sk_ref.3) | copy-start | bytes 196612
  6.6 238.8 %all-gather.2.cloned.1.call-start = ((), (), s32[]{:S(2)}) async-start(), calls=%async_computation | async-start | bytes 20971520 | tf_op jit(solution)/shard_map/all_gather | solution.py:464
  7.3 341.5 %all-reduce.3.cloned.1.call-start = ((), (), s32[]{:S(2)}) async-start(), calls=%async_computation.1 | async-start | bytes 8388608 | tf_op jit(solution)/shard_map/psum | solution.py:466
  96.1 1.6 copy-start.3
  97.8 1.6 copy-start.4
  99.4 1.6 copy-start.5
  101.0 0.8 copy-start.8
  101.9 0.7 copy-start.9
  176.6 3.7 %copy-start.1 = (bf16[16,2,2,144,512]{4,3,2,1,0:T(8,128)(2,1)S(1)}, bf16[16,2,2,144,512]{4,3,2,1,0:T(8,128)(2,1)}, u32[]{:S(2)}) copy-start(bf16[16,2,2,144,512]{4,3,2,1,0:T(8,128)(2,1)} %attend.1.part_ref) | copy-start | bytes 28311556
Sparse Core Ops, SparseCore 0:
  9.0 198.2 all-gather.1
  257.3 91.3 all-reduce.2

commit v2 on v1

--- a/solution.py
+++ b/solution.py
@@ -10,6 +10,7 @@
 HD = 128
 BLK = 128
 NEG = -1e30
+VMEM = 62 * 2**20
 MESH = pl.DeviceIdType.MESH
 BF16 = jnp.bfloat16
 F32 = jnp.float32
@@ -27,8 +28,8 @@
     return ((z + 4) % 4, ((x + 4) % 4) * 2 + c, (y + 4) % 4)
 
 
-def gather_kernel(q_ref, ck_ref, cv_ref, sk_ref, sv_ref, tab_ref,
-                  qall_ref, pk_ref, pv_ref, prev_ref, taball_ref,
+def gather_kernel(q_ref, ck_ref, cv_ref, sk_ref, sv_ref, tab_ref, wo_ref,
+                  qall_ref, pk_ref, pv_ref, prev_ref, taball_ref, won_ref,
                   send_sem, recv_sem, loc_sem):
     z, x, c, y = position()
     far_z, far_x = (z, x + jnp.where(c == 0, -1, 1))
@@ -40,7 +41,9 @@
         pl.semaphore_signal(barrier, inc=1, device_id=dev(z + off // 4, x + off % 4, c, y), device_id_type=MESH)
     pl.semaphore_signal(barrier, inc=1, device_id=dev(z, x, 1 - c, y), device_id_type=MESH)
     pl.semaphore_signal(barrier, inc=1, device_id=dev(far_z, far_x, 1 - c, y), device_id_type=MESH)
-    pl.semaphore_wait(barrier, 17)
+    for d in (1, -1):
+        pl.semaphore_signal(barrier, inc=1, device_id=dev(z, x, c, y + d), device_id_type=MESH)
+    pl.semaphore_wait(barrier, 19)
 
     copies = []
 
@@ -92,6 +95,10 @@
 
     own(0)
     own(1)
+    depth = wo_ref.shape[0] // 2
+    share = pl.ds(pl.multiple_of(c * depth, depth), depth)
+    wo_up = send(wo_ref.at[share], won_ref.at[0, share], dev(z, x, c, y + 1))
+    wo_down = send(wo_ref.at[share], won_ref.at[1, share], dev(z, x, c, y - 1))
     partner = dev(z, x, 1 - c, y)
     send(ck_ref, pk_ref, partner)
     send(cv_ref, pv_ref, partner)
@@ -126,7 +133,11 @@
                 ring[color, "b", a, d].wait_recv()
                 part = chunk(color, a, -d, 0 if d == 1 else 1)
                 ring[color, "c", a, d] = send(part, part, to(color, 0, d))
-    waited = {id(v) for k, v in ring.items() if k[1] != "c"}
+    wo_up.wait_recv()
+    send(won_ref.at[0, share], won_ref.at[0, share], partner)
+    wo_down.wait_recv()
+    send(won_ref.at[1, share], won_ref.at[1, share], partner)
+    waited = {id(v) for k, v in ring.items() if k[1] != "c"} | {id(wo_up), id(wo_down)}
     for cp in copies:
         if id(cp) not in waited:
             cp.wait_recv()
@@ -136,10 +147,10 @@
         cp.wait()
 
 
-N_GATHER = 15 + 2 + 8 + 2 + 4 + 8 + 4 + 4 + 12
-
-
-def gather_queries(q, ck, cv, sk, sv, tab):
+N_GATHER = 15 + 2 + 8 + 2 + 2 + 4 + 8 + 4 + 4 + 12 + 2
+
+
+def gather_queries(q, ck, cv, sk, sv, tab, wo):
     anyspec = pl.BlockSpec(memory_space=pl.ANY)
     return pl.pallas_call(
         gather_kernel,
@@ -149,21 +160,22 @@
             jax.ShapeDtypeStruct(cv.shape, BF16),
             jax.ShapeDtypeStruct((2, BLK, HD), BF16),
             jax.ShapeDtypeStruct(tab.shape, jnp.int32),
+            jax.ShapeDtypeStruct((2,) + wo.shape, BF16),
         ),
-        in_specs=[anyspec] * 6,
-        out_specs=[anyspec] * 5,
+        in_specs=[anyspec] * 7,
+        out_specs=[anyspec] * 6,
         scratch_shapes=[
             pltpu.SemaphoreType.DMA((N_GATHER,)),
             pltpu.SemaphoreType.DMA((N_GATHER,)),
             pltpu.SemaphoreType.DMA((2,)),
         ],
-        compiler_params=pltpu.CompilerParams(collective_id=0, has_side_effects=True),
+        compiler_params=pltpu.CompilerParams(collective_id=0, has_side_effects=True, vmem_limit_bytes=VMEM),
         name="gather_queries",
-    )(q, ck, cv, sk, sv, tab)
+    )(q, ck, cv, sk, sv, tab, wo)
 
 
 def attend_kernel(tab_ref, q_ref, ck_ref, cv_ref, pk_ref, pv_ref, sk_ref, sv_ref, prev_ref, out_ref,
-                  kall, vall, span, qt, m_s, l_s, acc, sems):
+                  kall, vall, span, sbuf, pbuf, m_s, l_s, acc, sems):
     i = pl.program_id(0)
     z, x, c, y = position()
     chip = i // 2
@@ -188,8 +200,6 @@
             cp.wait()
 
     heads = q_ref.shape[-1] // HD
-    for g in range(heads):
-        qt[:, g * HD:(g + 1) * HD] = q_ref[0, 0, :, g * HD:(g + 1) * HD].T
     m_s[...] = jnp.full_like(m_s, NEG)
     l_s[...] = jnp.zeros_like(l_s)
     acc[...] = jnp.zeros_like(acc)
@@ -197,18 +207,26 @@
     width = 256
 
     def pair(keys, values, bias):
-        for t in range(heads * HD // width):
-            cols = slice(t * width, (t + 1) * width)
-            s = jnp.dot(keys, qt[:, cols], preferred_element_type=F32) * scale
+        rows = keys.shape[0]
+        spans = [slice(t * width, (t + 1) * width) for t in range(heads * HD // width)]
+        tops = []
+        for cols in spans:
+            s = jnp.dot(keys, q_ref[0, 0, :, cols], preferred_element_type=F32) * scale
             if bias is not None:
                 s = s + bias
-            top = jnp.maximum(m_s[:, cols], jnp.max(s, axis=0, keepdims=True))
+            sbuf[0:rows, cols] = s
+            tops.append(jnp.maximum(m_s[:, cols], jnp.max(s, axis=0, keepdims=True)))
+        olds = []
+        for cols, top in zip(spans, tops):
             old = jnp.exp2(m_s[:, cols] - top)
-            p = jnp.exp2(s - top)
+            p = jnp.exp2(sbuf[0:rows, cols] - top)
+            pbuf[0:rows, cols] = p.astype(BF16)
             m_s[:, cols] = top
             l_s[:, cols] = l_s[:, cols] * old + jnp.sum(p, axis=0, keepdims=True)
+            olds.append(old)
+        for cols, old in zip(spans, olds):
             acc[:, cols] = acc[:, cols] * old + lax.dot_general(
-                values, p.astype(BF16), (((0,), (0,)), ((), ())), preferred_element_type=F32)
+                values, pbuf[0:rows, cols], (((0,), (0,)), ((), ())), preferred_element_type=F32)
 
     count = tab_ref[chip, 0, color * 16 + 15]
     base = color * 16
@@ -269,14 +287,15 @@
                 pltpu.VMEM((128, BLK, HD), BF16),
                 pltpu.VMEM((128, BLK, HD), BF16),
                 pltpu.VMEM((2, 3 * BLK, HD), BF16),
-                pltpu.VMEM((HD, width), BF16),
+                pltpu.VMEM((2 * BLK, width), F32),
+                pltpu.VMEM((2 * BLK, width), BF16),
                 pltpu.VMEM((1, width), F32),
                 pltpu.VMEM((1, width), F32),
                 pltpu.VMEM((HD, width), F32),
                 pltpu.SemaphoreType.DMA((8,)),
             ],
         ),
-        compiler_params=pltpu.CompilerParams(vmem_limit_bytes=40 * 2**20),
+        compiler_params=pltpu.CompilerParams(vmem_limit_bytes=VMEM),
         cost_estimate=pl.CostEstimate(flops=7_000_000_000, bytes_accessed=26_000_000, transcendentals=13_000_000),
         name="attend",
     )(tab, q_all, ck, cv, pk, pv, sk, sv, prev)
@@ -312,11 +331,15 @@
     dst[HD:HD + 16, :] = jnp.where(row == 0, hi, jnp.where(row == 1, mid, jnp.where(row == 2, low, 0.0))).astype(BF16)
 
 
-def reduce_kernel(part_ref, out_ref, loc, recv, send_sem, recv_sem, load_sem):
+def reduce_kernel(part_ref, won_ref, out_ref, woo_ref, loc, recv, send_sem, recv_sem, load_sem, wo_send, wo_recv):
     z, x, c, y = position()
     barrier = pltpu.get_barrier_semaphore()
     for dz, dx in ((0, 1), (0, -1), (1, 0), (-1, 0)):
         pl.semaphore_signal(barrier, inc=1, device_id=dev(z + dz, x + dx, c, y), device_id_type=MESH)
+    for d in (1, -1):
+        pl.semaphore_signal(barrier, inc=1, device_id=dev(z, x, c, y + d), device_id_type=MESH)
+    partner = dev(z, x, 1 - c, y)
+    pl.semaphore_signal(barrier, inc=1, device_id=partner, device_id_type=MESH)
 
     def step(color, a, b):
         return (a, b) if color == 0 else (b, a)
@@ -340,7 +363,21 @@
                 cp.start()
                 loads[color, a, b] = cp
                 k += 1
-    pl.semaphore_wait(barrier, 4)
+    pl.semaphore_wait(barrier, 7)
+
+    quarter = woo_ref.shape[0] // 4
+    wo_copies = []
+
+    def send_wo(src, k, target):
+        rows = pl.ds(pl.multiple_of(c * (2 * quarter) + (k % 2) * quarter, quarter), quarter)
+        cp = pltpu.make_async_remote_copy(
+            src_ref=src.at[rows], dst_ref=woo_ref.at[rows], send_sem=wo_send.at[k], recv_sem=wo_recv.at[k],
+            device_id=target, device_id_type=MESH)
+        cp.start()
+        wo_copies.append(cp)
+
+    send_wo(won_ref.at[0], 0, dev(z, x, c, y + 1))
+    send_wo(won_ref.at[1], 1, dev(z, x, c, y - 1))
 
     copies = {}
 
@@ -393,6 +430,9 @@
                 send((color, 2, "p1"), piece(color, 0, 1, 1), to(color, 0, 1))
             if b == 3:
                 send((color, 2, "m0"), piece(color, 0, 3, 0), to(color, 0, -1))
+    for k in (0, 1):
+        wo_copies[k].wait_recv()
+        send_wo(woo_ref, 2 + k, partner)
     for color in (0, 1):
         r = got((color, 2, "op"))
         merge(piece(color, 0, 1, 0), piece(color, 0, 1, 0), r)
@@ -412,29 +452,300 @@
                 out_ref[color * BLK:(color + 1) * BLK, col:col + HD] = own[0:HD, g * HD:(g + 1) * HD].T
     for cp, _ in copies.values():
         cp.wait_send()
+    for k in (2, 3):
+        wo_copies[k].wait_recv()
+    for cp in wo_copies:
+        cp.wait_send()
 
 
 N_REDUCE = 60
 
 
-def reduce_partials(part):
+def reduce_partials(part, won):
     rows, lanes = part.shape[-2:]
     return pl.pallas_call(
         reduce_kernel,
-        out_shape=jax.ShapeDtypeStruct((2 * BLK, 2 * lanes), BF16),
-        in_specs=[pl.BlockSpec(memory_space=pl.ANY)],
-        out_specs=pl.BlockSpec(memory_space=pltpu.VMEM),
+        out_shape=(jax.ShapeDtypeStruct((2 * BLK, 2 * lanes), BF16),
+                   jax.ShapeDtypeStruct(won.shape[1:], BF16)),
+        in_specs=[pl.BlockSpec(memory_space=pl.ANY)] * 2,
+        out_specs=(pl.BlockSpec(memory_space=pltpu.VMEM), pl.BlockSpec(memory_space=pl.ANY)),
         scratch_shapes=[
             pltpu.VMEM((2, 16, 2, rows, lanes), BF16),
             pltpu.VMEM((N_REDUCE, rows, lanes), BF16),
             pltpu.SemaphoreType.DMA((N_REDUCE,)),
             pltpu.SemaphoreType.DMA((N_REDUCE,)),
             pltpu.SemaphoreType.DMA((32,)),
+            pltpu.SemaphoreType.DMA((4,)),
+            pltpu.SemaphoreType.DMA((4,)),
         ],
         compiler_params=pltpu.CompilerParams(
-            collective_id=1, has_side_effects=True, vmem_limit_bytes=40 * 2**20),
+            collective_id=1, has_side_effects=True, vmem_limit_bytes=VMEM),
         name="reduce_partials",
-    )(part)
+    )(part, won)
+
+
+NCH = 4
+
+
+def project_kernel(att_ref, wo_ref, won_ref, woo_ref, out_ref,
+                   attz, hb, relay, w, acc, tile, zrelay,
+                   w_sem, a_send, a_recv, b_send, b_recv, s_send, s_recv, t_send, t_recv, home_sem):
+    z, x, c, y = position()
+    barrier = pltpu.get_barrier_semaphore()
+    for d in (1, -1):
+        pl.semaphore_signal(barrier, inc=1, device_id=dev(z + d, x, c, y), device_id_type=MESH)
+        pl.semaphore_signal(barrier, inc=1, device_id=dev(z, x, c, y + d), device_id_type=MESH)
+    loads = [
+        pltpu.make_async_copy(wo_ref, w.at[0], w_sem.at[0]),
+        pltpu.make_async_copy(won_ref.at[1], w.at[1], w_sem.at[1]),
+        pltpu.make_async_copy(won_ref.at[0], w.at[3], w_sem.at[2]),
+        pltpu.make_async_copy(woo_ref, w.at[2], w_sem.at[3]),
+    ]
+    for cp in loads:
+        cp.start()
+    pl.semaphore_wait(barrier, 4)
+
+    tokens, depth = att_ref.shape
+    half = tokens // 2
+    cols = wo_ref.shape[1]
+    lo, hi = pl.ds(0, half), pl.ds(half, half)
+
+    def remote(src, dst, ssem, rsem, target):
+        return pltpu.make_async_remote_copy(
+            src_ref=src, dst_ref=dst, send_sem=ssem, recv_sem=rsem, device_id=target, device_id_type=MESH)
+
+    zp, zm = dev(z + 1, x, c, y), dev(z - 1, x, c, y)
+    yp, ym = dev(z, x, c, y + 1), dev(z, x, c, y - 1)
+
+    ring = [
+        remote(att_ref, attz.at[3], a_send.at[0], a_recv.at[0], zp),
+        remote(att_ref, attz.at[1], a_send.at[1], a_recv.at[1], zm),
+        remote(attz.at[3, lo], attz.at[2, lo], a_send.at[2], a_recv.at[2], zp),
+        remote(attz.at[1, hi], attz.at[2, hi], a_send.at[3], a_recv.at[3], zm),
+    ]
+    ring[0].start()
+    ring[1].start()
+
+    def spread(src):
+        return [
+            remote(src, hb.at[3], b_send.at[0], b_recv.at[0], yp),
+            remote(src, hb.at[1], b_send.at[1], b_recv.at[1], ym),
+            remote(src.at[lo], relay.at[0], b_send.at[2], b_recv.at[2], yp),
+            remote(src.at[hi], relay.at[1], b_send.at[3], b_recv.at[3], ym),
+        ]
+
+    for dz in (0, 3, 1, 2):
+        if dz == 3:
+            ring[0].wait_recv()
+            ring[2].start()
+        if dz == 1:
+            ring[1].wait_recv()
+            ring[3].start()
+        if dz == 2:
+            ring[2].wait_recv()
+            ring[3].wait_recv()
+        src = att_ref if dz == 0 else attz.at[dz]
+        d = (dz - y + 4) % 4
+        sends = spread(src)
+
+        @pl.when(d == 0)
+        def _():
+            hb[0] = src[...]
+
+        @pl.when(d == 1)
+        def _():
+            sends[0].start()
+
+        @pl.when(d == 3)
+        def _():
+            sends[1].start()
+
+        @pl.when(d == 2)
+        def _():
+            sends[2].start()
+            sends[3].start()
+
+    sends = spread(att_ref)
+    onward = [
+        remote(relay.at[0], hb.at[2, lo], b_send.at[4], b_recv.at[4], yp),
+        remote(relay.at[1], hb.at[2, hi], b_send.at[5], b_recv.at[5], ym),
+    ]
+    step = cols // NCH
+
+    def term(r, first):
+        def one(k, carry):
+            sl = pl.ds(pl.multiple_of(k * 256, 256), 256)
+            v = jnp.dot(hb[r], w[r, :, sl], preferred_element_type=F32)
+            acc[:, sl] = v if first else acc[:, sl] + v
+            return carry
+        lax.fori_loop(0, cols // 256, one, 0)
+
+    loads[0].wait()
+    term(0, True)
+    for k in (0, 1):
+        sends[2 + k].wait_recv()
+        onward[k].start()
+    sends[0].wait_recv()
+    loads[2].wait()
+    term(3, False)
+    sends[1].wait_recv()
+    loads[1].wait()
+    term(1, False)
+    onward[0].wait_recv()
+    onward[1].wait_recv()
+    loads[3].wait()
+
+    def region(ref, f, ch, rows=None):
+        sl = pl.ds(pl.multiple_of(((f + 8) % 4) * cols + ch * step, step), step)
+        return ref.at[:, sl] if rows is None else ref.at[rows, sl]
+
+    def shifts(ch):
+        n = ch * 5
+        src = tile.at[ch]
+        return [
+            remote(src, region(out_ref, z, ch), s_send.at[n], s_recv.at[n], zp),
+            remote(src, region(out_ref, z, ch), s_send.at[n], s_recv.at[n], zm),
+            remote(src.at[lo], zrelay.at[ch, 0], s_send.at[n + 1], s_recv.at[n + 1], zp),
+            remote(src.at[hi], zrelay.at[ch, 1], s_send.at[n + 2], s_recv.at[n + 2], zm),
+            remote(zrelay.at[ch, 0], region(out_ref, z - 1, ch, lo), s_send.at[n + 3], s_recv.at[n + 3], zp),
+            remote(zrelay.at[ch, 1], region(out_ref, z + 1, ch, hi), s_send.at[n + 4], s_recv.at[n + 4], zm),
+        ]
+
+    def home(ch):
+        return pltpu.make_async_copy(tile.at[ch], region(out_ref, z, ch), home_sem.at[ch])
+
+    def bcast(ch):
+        n = ch * 4
+        mine = region(out_ref, z - y, ch)
+        up = region(out_ref, z - y + 1, ch, lo)
+        down = region(out_ref, z - y - 1, ch, hi)
+        return [
+            remote(mine, mine, t_send.at[n], t_recv.at[n], yp),
+            remote(mine, mine, t_send.at[n + 1], t_recv.at[n + 1], ym),
+            remote(up, up, t_send.at[n + 2], t_recv.at[n + 2], yp),
+            remote(down, down, t_send.at[n + 3], t_recv.at[n + 3], ym),
+        ]
+
+    for t in range(NCH + 3):
+        if t < NCH:
+            for k in range(step // 256):
+                sl = slice(t * step + k * 256, t * step + (k + 1) * 256)
+                v = acc[:, sl] + jnp.dot(hb[2], w[2, :, sl], preferred_element_type=F32)
+                tile[t, :, k * 256:(k + 1) * 256] = v.astype(BF16)
+            sh = shifts(t)
+
+            @pl.when(y == 0)
+            def _():
+                home(t).start()
+
+            @pl.when(y == 1)
+            def _():
+                sh[0].start()
+
+            @pl.when(y == 3)
+            def _():
+                sh[1].start()
+
+            @pl.when(y == 2)
+            def _():
+                sh[2].start()
+                sh[3].start()
+        if 1 <= t < NCH + 1:
+            sr = shifts(t - 1)
+
+            @pl.when(y == 2)
+            def _():
+                sr[2].wait_recv()
+                sr[4].start()
+                sr[3].wait_recv()
+                sr[5].start()
+        if 2 <= t < NCH + 2:
+            se = shifts(t - 2)
+
+            @pl.when(y == 0)
+            def _():
+                home(t - 2).wait()
+
+            @pl.when(y % 2 == 1)
+            def _():
+                se[0].wait_recv()
+
+            @pl.when(y == 2)
+            def _():
+                se[4].wait_recv()
+                se[5].wait_recv()
+
+            b = bcast(t - 2)
+            b[0].start()
+            b[1].start()
+        if 3 <= t:
+            b = bcast(t - 3)
+            b[0].wait_recv()
+            b[2].start()
+            b[1].wait_recv()
+            b[3].start()
+    for ch in range(NCH):
+        b = bcast(ch)
+        b[2].wait_recv()
+        b[3].wait_recv()
+        for cp in b:
+            cp.wait_send()
+        sw = shifts(ch)
+
+        @pl.when(y % 2 == 1)
+        def _():
+            sw[0].wait_send()
+
+        @pl.when(y == 2)
+        def _():
+            for cp in sw[2:]:
+                cp.wait_send()
+    for cp in ring + sends + onward:
+        cp.wait_send()
+
+
+def project(att, wo, won, woo):
+    tokens, depth = att.shape
+    cols = wo.shape[1]
+    anyspec = pl.BlockSpec(memory_space=pl.ANY)
+    sem = pltpu.SemaphoreType.DMA
+    return pl.pallas_call(
+        project_kernel,
+        out_shape=jax.ShapeDtypeStruct((tokens, 4 * cols), BF16),
+        in_specs=[pl.BlockSpec(memory_space=pltpu.VMEM)] + [anyspec] * 3,
+        out_specs=anyspec,
+        scratch_shapes=[
+            pltpu.VMEM((4, tokens, depth), BF16),
+            pltpu.VMEM((4, tokens, depth), BF16),
+            pltpu.VMEM((2, tokens // 2, depth), BF16),
+            pltpu.VMEM((4, depth, cols), BF16),
+            pltpu.VMEM((tokens, cols), F32),
+            pltpu.VMEM((NCH, tokens, cols // NCH), BF16),
+            pltpu.VMEM((NCH, 2, tokens // 2, cols // NCH), BF16),
+            sem((4,)), sem((4,)), sem((4,)), sem((6,)), sem((6,)),
+            sem((5 * NCH,)), sem((5 * NCH,)), sem((4 * NCH,)), sem((4 * NCH,)), sem((NCH,)),
+        ],
+        compiler_params=pltpu.CompilerParams(
+            collective_id=2, has_side_effects=True, vmem_limit_bytes=VMEM),
+        name="project",
+    )(att, wo, won, woo)
+
+
+def turn_kernel(q_ref, out_ref):
+    for color in range(2):
+        for g in range(q_ref.shape[1] // HD):
+            out_ref[color, :, g * BLK:(g + 1) * BLK] = q_ref[color * BLK:(color + 1) * BLK, g * HD:(g + 1) * HD].T
+
+
+def turn(queries):
+    return pl.pallas_call(
+        turn_kernel,
+        out_shape=jax.ShapeDtypeStruct((2, HD, queries.shape[1]), BF16),
+        in_specs=[pl.BlockSpec(memory_space=pltpu.VMEM)],
+        out_specs=pl.BlockSpec(memory_space=pltpu.VMEM),
+        compiler_params=pltpu.CompilerParams(vmem_limit_bytes=VMEM),
+        name="turn",
+    )(queries)
 
 
 def request_table(block_slot, pattern, core, cb_local):
@@ -456,14 +767,11 @@
 def body(queries, span_k, span_v, cache_k, cache_v, block_slot, pattern, wo):
     core = lax.axis_index("seq") % 2
     tab = request_table(block_slot, pattern, core, cache_k.shape[0])
-    q = queries.reshape(2, BLK, queries.shape[1])
-    q_all, pk, pv, prev, tab_all = gather_queries(q, cache_k, cache_v, span_k, span_v, tab)
+    q = turn(queries)
+    q_all, pk, pv, prev, tab_all, won = gather_queries(q, cache_k, cache_v, span_k, span_v, tab, wo)
     part = attend(tab_all, q_all, cache_k, cache_v, pk, pv, span_k, span_v, prev)
-    attended = reduce_partials(part)
-    partial_terms = jnp.dot(
-        attended, lax.all_gather(wo, "fsdp", axis=1, tiled=True), preferred_element_type=F32
-    )
-    return lax.psum(partial_terms.astype(BF16), "head")
+    attended, woo = reduce_partials(part, won)
+    return project(attended, wo, won, woo)
 
 
 def solution(mesh):

time: 361 us -> 266 us (0.74)
  waiting for transfers between devices: 92.3 us -> 0 us
  Pallas kernels: 225 us -> 255 us
  between operations: 13.6 us -> 0.07 us
  matrix products: 11.9 us -> 0 us
  local copies, waits for them, and re-layouts: 16.8 us -> 6.65 us
    psum x1 -> x0, waiting for transfers between devices: 91.6 us -> none  [body(): return lax.psum(partial_terms.astype(BF16), 'head')]
    pallas_call x1 -> x3, Pallas kernels: 65 us -> 144 us  [the longest x1 85.1 us: project(): pl.pallas_call(project_kernel, out_shape=jax.ShapeDtypeStruct((tokens, 4...]
    pallas_call x1, Pallas kernels: 74 us -> 47.6 us  [attend(): pl.pallas_call(attend_kernel, out_shape=jax.ShapeDtypeStruct((16, 2, 2, H...]
    pallas_call x1, Pallas kernels: 85.7 us -> 63.6 us  [gather_queries(): pl.pallas_call(gather_kernel, out_shape=(jax.ShapeDtypeStruct((16, 2, BLK...]
    dot_general x1 -> x0, matrix products: 11.9 us -> none  [body(): jnp.dot(attended, lax.all_gather(wo, 'fsdp', axis=1, tiled=True), preferr...]
    unnamed x23 -> x3, local copies, waits for them, and re-layouts: 14.8 us -> 4.64 us
  transfers between devices with their start and end apart: 2 -> 0, of which waited for: 1 -> 0; matrix products, arithmetic and copies ran while one was open for 1% -> 0% of each run, Pallas kernels for 62% -> 0%
where the time goes in v2:
time: 266 us; the launch traced here: 264 us
  Pallas kernels  255 us (96%)
  local copies, waits for them, and re-layouts  6.65 us (2%)
    pallas_call x1, Pallas kernels, project(): pl.pallas_call(project_kernel, out_shape=jax.ShapeDtypeStruct((tokens, 4...  85.1 us
    pallas_call x1, Pallas kernels, gather_queries(): pl.pallas_call(gather_kernel, out_shape=(jax.ShapeDtypeStruct((16, 2, BLK...  63.6 us
    pallas_call x1, Pallas kernels, reduce_partials(): pl.pallas_call(reduce_kernel, out_shape=(jax.ShapeDtypeStruct((2 * BLK, 2...  56.9 us
    pallas_call x1, Pallas kernels, attend(): pl.pallas_call(attend_kernel, out_shape=jax.ShapeDtypeStruct((16, 2, 2, H...  47.6 us

profile of v2, /device:TPU:0, one launch (start us, length us, event | category | flops | bytes accessed | tf_op | source)
XLA Modules:
  0.0 263.6 jit_solution(15406629186734722880)
XLA Ops:
  0.0 0.0 copy-start
  0.0 0.7 compare_select_fusion
  0.7 0.1 reshape.164
  0.8 0.0 copy-done
  0.8 1.1 gather_fusion
  1.9 0.1 reshape.163
  2.1 0.2 convert_reduce_fusion
  2.3 0.7 select_reduce_fusion
  3.0 0.1 reshape.161
  3.1 0.6 pad.4.tab_ref
  3.7 2.0 turn.1.q_ref
  5.7 63.6 %gather_queries.1 = (bf16[16,2,128,1024]{3,2,1,0:T(8,128)(2,1)}, bf16[64,128,128]{2,1,0:T(8,128)(2,1)}, bf16[64,128,128]{2,1,0:T(8,128)(2,1)}, bf16[2,128,128]{2...) custom-call(bf16[2,128,1024]{2,1,0:T(8,128)(2,1)} %turn.1.q_ref, bf16[64,128,128]{2,1,0:T(8,128)(2,1)} %ck_ref.3, ...), custom_call_target="tpu_custom_call" | custom-call | tf_op jit(solution)/shard_map/gather_queries/pallas_call | solution.py:155
  69.4 47.6 %attend.1.part_ref = bf16[16,2,2,144,512]{4,3,2,1,0:T(8,128)(2,1)} custom-call(s32[16,1,128]{2,1,0:T(1,128)} %get-tuple-element.13.tab_ref, bf16[16,2,128,1024]{3,2,1,0:T(8,128)(2,1)} %get-tuple-element.14.q_ref, bf16[64,128,128]{2,1,0:T(8,128)(2,1)} %ck_ref.3, bf16[64,128,128]{2,1,0:T(8,128)(2,1)} %cv_ref.3, ...), custom_call_target="tpu_custom_call" | custom-call | flops 7000000000 | bytes 26000000 | tf_op jit(solution)/shard_map/attend/pallas_call | solution.py:278
  117.0 56.9 %reduce_partials.1 = (bf16[256,1024]{1,0:T(8,128)(2,1)}, bf16[1024,2048]{1,0:T(8,128)(2,1)}) custom-call(bf16[16,2,2,144,512]{4,3,2,1,0:T(8,128)(2,1)} %attend.1.part_ref, bf16[2,1024,2048]{2,1,0:T(8,128)(2,1)} %get-tuple-element.18.won_ref), custom_call_target="tpu_custom_call" | custom-call | tf_op jit(solution)/shard_map/reduce_partials/pallas_call | solution.py:466
  173.9 85.1 %project.1 = bf16[256,8192]{1,0:T(8,128)(2,1)} custom-call(bf16[256,1024]{1,0:T(8,128)(2,1)} %get-tuple-element.19.att_ref, bf16[1024,2048]{1,0:T(8,128)(2,1)} %wo_ref.3, bf16[2,1024,2048]{2,1,0:T(8,128)(2,1)} %get-tuple-element.18.won_ref, bf16[1024,2048]{1,0:T(8,128)(2,1)} %get-tuple-element.20.woo_ref), custom_call_target="tpu_custom_call" | custom-call | tf_op jit(solution)/shard_map/project/pallas_call | solution.py:712
  259.0 4.6 %copy.10 = bf16[256,8192]{1,0:T(8,128)(2,1)} copy(bf16[256,8192]{1,0:T(8,128)(2,1)} %project.1) | data formatting | bytes 8388608
  (7 shorter events, 0.1 us)
Async XLA Ops:
  0.0 0.8 copy-start

commit v3 on v1

--- a/solution.py
+++ b/solution.py
@@ -10,6 +10,7 @@
 HD = 128
 BLK = 128
 NEG = -1e30
+VMEM = 62 * 2**20
 MESH = pl.DeviceIdType.MESH
 BF16 = jnp.bfloat16
 F32 = jnp.float32
@@ -27,8 +28,8 @@
     return ((z + 4) % 4, ((x + 4) % 4) * 2 + c, (y + 4) % 4)
 
 
-def gather_kernel(q_ref, ck_ref, cv_ref, sk_ref, sv_ref, tab_ref,
-                  qall_ref, pk_ref, pv_ref, prev_ref, taball_ref,
+def gather_kernel(q_ref, ck_ref, cv_ref, sk_ref, sv_ref, tab_ref, wo_ref,
+                  qall_ref, pk_ref, pv_ref, prev_ref, taball_ref, won_ref,
                   send_sem, recv_sem, loc_sem):
     z, x, c, y = position()
     far_z, far_x = (z, x + jnp.where(c == 0, -1, 1))
@@ -40,7 +41,9 @@
         pl.semaphore_signal(barrier, inc=1, device_id=dev(z + off // 4, x + off % 4, c, y), device_id_type=MESH)
     pl.semaphore_signal(barrier, inc=1, device_id=dev(z, x, 1 - c, y), device_id_type=MESH)
     pl.semaphore_signal(barrier, inc=1, device_id=dev(far_z, far_x, 1 - c, y), device_id_type=MESH)
-    pl.semaphore_wait(barrier, 17)
+    for d in (1, -1):
+        pl.semaphore_signal(barrier, inc=1, device_id=dev(z, x, c, y + d), device_id_type=MESH)
+    pl.semaphore_wait(barrier, 19)
 
     copies = []
 
@@ -92,6 +95,10 @@
 
     own(0)
     own(1)
+    depth = wo_ref.shape[0] // 2
+    share = pl.ds(pl.multiple_of(c * depth, depth), depth)
+    wo_up = send(wo_ref.at[share], won_ref.at[0, share], dev(z, x, c, y + 1))
+    wo_down = send(wo_ref.at[share], won_ref.at[1, share], dev(z, x, c, y - 1))
     partner = dev(z, x, 1 - c, y)
     send(ck_ref, pk_ref, partner)
     send(cv_ref, pv_ref, partner)
@@ -126,7 +133,11 @@
                 ring[color, "b", a, d].wait_recv()
                 part = chunk(color, a, -d, 0 if d == 1 else 1)
                 ring[color, "c", a, d] = send(part, part, to(color, 0, d))
-    waited = {id(v) for k, v in ring.items() if k[1] != "c"}
+    wo_up.wait_recv()
+    send(won_ref.at[0, share], won_ref.at[0, share], partner)
+    wo_down.wait_recv()
+    send(won_ref.at[1, share], won_ref.at[1, share], partner)
+    waited = {id(v) for k, v in ring.items() if k[1] != "c"} | {id(wo_up), id(wo_down)}
     for cp in copies:
         if id(cp) not in waited:
             cp.wait_recv()
@@ -136,10 +147,10 @@
         cp.wait()
 
 
-N_GATHER = 15 + 2 + 8 + 2 + 4 + 8 + 4 + 4 + 12
-
-
-def gather_queries(q, ck, cv, sk, sv, tab):
+N_GATHER = 15 + 2 + 8 + 2 + 2 + 4 + 8 + 4 + 4 + 12 + 2
+
+
+def gather_queries(q, ck, cv, sk, sv, tab, wo):
     anyspec = pl.BlockSpec(memory_space=pl.ANY)
     return pl.pallas_call(
         gather_kernel,
@@ -149,21 +160,22 @@
             jax.ShapeDtypeStruct(cv.shape, BF16),
             jax.ShapeDtypeStruct((2, BLK, HD), BF16),
             jax.ShapeDtypeStruct(tab.shape, jnp.int32),
+            jax.ShapeDtypeStruct((2,) + wo.shape, BF16),
         ),
-        in_specs=[anyspec] * 6,
-        out_specs=[anyspec] * 5,
+        in_specs=[anyspec] * 7,
+        out_specs=[anyspec] * 6,
         scratch_shapes=[
             pltpu.SemaphoreType.DMA((N_GATHER,)),
             pltpu.SemaphoreType.DMA((N_GATHER,)),
             pltpu.SemaphoreType.DMA((2,)),
         ],
-        compiler_params=pltpu.CompilerParams(collective_id=0, has_side_effects=True),
+        compiler_params=pltpu.CompilerParams(collective_id=0, has_side_effects=True, vmem_limit_bytes=VMEM),
         name="gather_queries",
-    )(q, ck, cv, sk, sv, tab)
+    )(q, ck, cv, sk, sv, tab, wo)
 
 
 def attend_kernel(tab_ref, q_ref, ck_ref, cv_ref, pk_ref, pv_ref, sk_ref, sv_ref, prev_ref, out_ref,
-                  kall, vall, span, qt, m_s, l_s, acc, sems):
+                  kall, vall, span, sbuf, pbuf, m_s, l_s, acc, sems):
     i = pl.program_id(0)
     z, x, c, y = position()
     chip = i // 2
@@ -188,8 +200,6 @@
             cp.wait()
 
     heads = q_ref.shape[-1] // HD
-    for g in range(heads):
-        qt[:, g * HD:(g + 1) * HD] = q_ref[0, 0, :, g * HD:(g + 1) * HD].T
     m_s[...] = jnp.full_like(m_s, NEG)
     l_s[...] = jnp.zeros_like(l_s)
     acc[...] = jnp.zeros_like(acc)
@@ -197,18 +207,26 @@
     width = 256
 
     def pair(keys, values, bias):
-        for t in range(heads * HD // width):
-            cols = slice(t * width, (t + 1) * width)
-            s = jnp.dot(keys, qt[:, cols], preferred_element_type=F32) * scale
+        rows = keys.shape[0]
+        spans = [slice(t * width, (t + 1) * width) for t in range(heads * HD // width)]
+        tops = []
+        for cols in spans:
+            s = jnp.dot(keys, q_ref[0, 0, :, cols], preferred_element_type=F32) * scale
             if bias is not None:
                 s = s + bias
-            top = jnp.maximum(m_s[:, cols], jnp.max(s, axis=0, keepdims=True))
+            sbuf[0:rows, cols] = s
+            tops.append(jnp.maximum(m_s[:, cols], jnp.max(s, axis=0, keepdims=True)))
+        olds = []
+        for cols, top in zip(spans, tops):
             old = jnp.exp2(m_s[:, cols] - top)
-            p = jnp.exp2(s - top)
+            p = jnp.exp2(sbuf[0:rows, cols] - top)
+            pbuf[0:rows, cols] = p.astype(BF16)
             m_s[:, cols] = top
             l_s[:, cols] = l_s[:, cols] * old + jnp.sum(p, axis=0, keepdims=True)
+            olds.append(old)
+        for cols, old in zip(spans, olds):
             acc[:, cols] = acc[:, cols] * old + lax.dot_general(
-                values, p.astype(BF16), (((0,), (0,)), ((), ())), preferred_element_type=F32)
+                values, pbuf[0:rows, cols], (((0,), (0,)), ((), ())), preferred_element_type=F32)
 
     count = tab_ref[chip, 0, color * 16 + 15]
     base = color * 16
@@ -269,14 +287,15 @@
                 pltpu.VMEM((128, BLK, HD), BF16),
                 pltpu.VMEM((128, BLK, HD), BF16),
                 pltpu.VMEM((2, 3 * BLK, HD), BF16),
-                pltpu.VMEM((HD, width), BF16),
+                pltpu.VMEM((2 * BLK, width), F32),
+                pltpu.VMEM((2 * BLK, width), BF16),
                 pltpu.VMEM((1, width), F32),
                 pltpu.VMEM((1, width), F32),
                 pltpu.VMEM((HD, width), F32),
                 pltpu.SemaphoreType.DMA((8,)),
             ],
         ),
-        compiler_params=pltpu.CompilerParams(vmem_limit_bytes=40 * 2**20),
+        compiler_params=pltpu.CompilerParams(vmem_limit_bytes=VMEM),
         cost_estimate=pl.CostEstimate(flops=7_000_000_000, bytes_accessed=26_000_000, transcendentals=13_000_000),
         name="attend",
     )(tab, q_all, ck, cv, pk, pv, sk, sv, prev)
@@ -312,129 +331,456 @@
     dst[HD:HD + 16, :] = jnp.where(row == 0, hi, jnp.where(row == 1, mid, jnp.where(row == 2, low, 0.0))).astype(BF16)
 
 
-def reduce_kernel(part_ref, out_ref, loc, recv, send_sem, recv_sem, load_sem):
+NCH = 4
+SECOND = (2, 1, 3, 0)
+
+
+def finish_kernel(part_ref, wo_ref, won_ref, out_ref,
+                  loc, recv, att, attz, hb, relay, w, acc, tile, zrelay,
+                  load_sem, r_send, r_recv, wo_send, wo_recv, w_sem,
+                  a_send, a_recv, b_send, b_recv, s_send, s_recv, t_send, t_recv, home_sem):
     z, x, c, y = position()
+    partner = dev(z, x, 1 - c, y)
+    zp, zm = dev(z + 1, x, c, y), dev(z - 1, x, c, y)
+    yp, ym = dev(z, x, c, y + 1), dev(z, x, c, y - 1)
     barrier = pltpu.get_barrier_semaphore()
-    for dz, dx in ((0, 1), (0, -1), (1, 0), (-1, 0)):
-        pl.semaphore_signal(barrier, inc=1, device_id=dev(z + dz, x + dx, c, y), device_id_type=MESH)
-
-    def step(color, a, b):
-        return (a, b) if color == 0 else (b, a)
-
-    def slot(color, a, b):
-        dz, dx = step(color, a, b)
-        return ((z + dz + 4) % 4) * 4 + (x + dx + 4) % 4
-
-    def to(color, a, b):
-        dz, dx = step(color, a, b)
+    for target in (zp, zm, dev(z, x + 1, c, y), dev(z, x - 1, c, y), yp, ym, partner):
+        pl.semaphore_signal(barrier, inc=1, device_id=target, device_id_type=MESH)
+
+    def remote(src, dst, ssem, rsem, target):
+        return pltpu.make_async_remote_copy(
+            src_ref=src, dst_ref=dst, send_sem=ssem, recv_sem=rsem, device_id=target, device_id_type=MESH)
+
+    def step(h, a, b):
+        return (a, b) if h == 0 else (b, a)
+
+    def to(h, a, b):
+        dz, dx = step(h, a, b)
         return dev(z + dz, x + dx, c, y)
 
-    order = [2, 1, 3, 0]
     loads = {}
-    k = 0
-    for a in (2, 1, 3, 0):
-        for b in order:
-            for color in (0, 1):
-                cp = pltpu.make_async_copy(
-                    part_ref.at[slot(color, a, b), color], loc.at[color, a * 4 + b], load_sem.at[k])
-                cp.start()
-                loads[color, a, b] = cp
-                k += 1
-    pl.semaphore_wait(barrier, 4)
-
+    for k in (0, 1):
+        for a in (2, 1, 3, 0):
+            for b in SECOND:
+                for h in (0, 1):
+                    dz, dx = step(h, a, b)
+                    slot = ((z + dz) % 4) * 4 + (x + dx) % 4
+                    cp = pltpu.make_async_copy(part_ref.at[slot, k, h], loc.at[k * 2 + h, a * 4 + b], load_sem.at[len(loads)])
+                    cp.start()
+                    loads[k, h, a, b] = cp
+    w_loads = [
+        pltpu.make_async_copy(wo_ref, w.at[0], w_sem.at[0]),
+        pltpu.make_async_copy(won_ref.at[1], w.at[1], w_sem.at[1]),
+        pltpu.make_async_copy(won_ref.at[0], w.at[3], w_sem.at[2]),
+    ]
+    for cp in w_loads:
+        cp.start()
+    pl.semaphore_wait(barrier, 7)
+
+    quarter = wo_ref.shape[0] // 4
+    wo_copies = []
+
+    def send_wo(src, n, target):
+        rows = pl.ds(pl.multiple_of(c * (2 * quarter) + (n % 2) * quarter, quarter), quarter)
+        cp = remote(src.at[rows], w.at[2, rows], wo_send.at[n], wo_recv.at[n], target)
+        cp.start()
+        wo_copies.append(cp)
+
+    send_wo(won_ref.at[0], 0, yp)
+    send_wo(won_ref.at[1], 1, ym)
+
+    quart = loc.shape[-1] // 2
     copies = {}
 
     def send(key, src, target):
-        k = len(copies)
-        cp = pltpu.make_async_remote_copy(
-            src_ref=src, dst_ref=recv.at[k], send_sem=send_sem.at[k], recv_sem=recv_sem.at[k],
-            device_id=target, device_id_type=MESH)
+        n = len(copies)
+        cp = remote(src, recv.at[n], r_send.at[n], r_recv.at[n], target)
         cp.start()
-        copies[key] = (cp, k)
+        copies[key] = (cp, n)
 
     def got(key):
-        cp, k = copies[key]
+        cp, n = copies[key]
         cp.wait_recv()
-        return recv.at[k]
-
-    def piece(color, a, b, half):
-        return loc.at[color, a * 4 + b, half]
-
-    for b in order:
-        for color in (0, 1):
-            loads[color, 2, b].wait()
-            send((color, 1, b, "op"), piece(color, 2, b, 0), to(color, 1, 0))
-            send((color, 1, b, "om"), piece(color, 2, b, 1), to(color, -1, 0))
-    for b in order:
-        for color in (0, 1):
-            loads[color, 1, b].wait()
-            send((color, 1, b, "p1"), piece(color, 1, b, 1), to(color, 1, 0))
-            loads[color, 3, b].wait()
-            send((color, 1, b, "m0"), piece(color, 3, b, 0), to(color, -1, 0))
-    for b in order:
-        for color in (0, 1):
-            r = got((color, 1, b, "op"))
-            merge(piece(color, 1, b, 0), piece(color, 1, b, 0), r)
-            send((color, 1, b, "p0"), piece(color, 1, b, 0), to(color, 1, 0))
-            r = got((color, 1, b, "om"))
-            merge(piece(color, 3, b, 1), piece(color, 3, b, 1), r)
-            send((color, 1, b, "m1"), piece(color, 3, b, 1), to(color, -1, 0))
-    for b in order:
-        for color in (0, 1):
-            loads[color, 0, b].wait()
-            for half in (0, 1):
-                p = got((color, 1, b, "p%d" % half))
-                m = got((color, 1, b, "m%d" % half))
-                merge(piece(color, 0, b, half), piece(color, 0, b, half), p, m)
+        return recv.at[n]
+
+    def piece(k, h, a, b, q):
+        return loc.at[k * 2 + h, a * 4 + b, :, q * quart:(q + 1) * quart]
+
+    def first_sends(k, b):
+        for h in (0, 1):
+            loads[k, h, 2, b].wait()
+            send((k, h, b, "op"), piece(k, h, 2, b, 0), to(h, 1, 0))
+            send((k, h, b, "om"), piece(k, h, 2, b, 1), to(h, -1, 0))
+
+    def first_raw(k, b):
+        for h in (0, 1):
+            loads[k, h, 1, b].wait()
+            send((k, h, b, "p1"), piece(k, h, 1, b, 1), to(h, 1, 0))
+            loads[k, h, 3, b].wait()
+            send((k, h, b, "m0"), piece(k, h, 3, b, 0), to(h, -1, 0))
+
+    def first_sums(k, b):
+        for h in (0, 1):
+            r = got((k, h, b, "op"))
+            merge(piece(k, h, 1, b, 0), piece(k, h, 1, b, 0), r)
+            send((k, h, b, "p0"), piece(k, h, 1, b, 0), to(h, 1, 0))
+            r = got((k, h, b, "om"))
+            merge(piece(k, h, 3, b, 1), piece(k, h, 3, b, 1), r)
+            send((k, h, b, "m1"), piece(k, h, 3, b, 1), to(h, -1, 0))
+
+    def second_sends(k, b):
+        for h in (0, 1):
+            loads[k, h, 0, b].wait()
+            for q in (1, 0):
+                p = got((k, h, b, "p%d" % q))
+                m = got((k, h, b, "m%d" % q))
+                merge(piece(k, h, 0, b, q), piece(k, h, 0, b, q), p, m)
             if b == 2:
-                send((color, 2, "op"), piece(color, 0, 2, 0), to(color, 0, 1))
-                send((color, 2, "om"), piece(color, 0, 2, 1), to(color, 0, -1))
+                send((k, h, "op"), piece(k, h, 0, 2, 0), to(h, 0, 1))
+                send((k, h, "om"), piece(k, h, 0, 2, 1), to(h, 0, -1))
             if b == 1:
-                send((color, 2, "p1"), piece(color, 0, 1, 1), to(color, 0, 1))
+                send((k, h, "p1"), piece(k, h, 0, 1, 1), to(h, 0, 1))
             if b == 3:
-                send((color, 2, "m0"), piece(color, 0, 3, 0), to(color, 0, -1))
-    for color in (0, 1):
-        r = got((color, 2, "op"))
-        merge(piece(color, 0, 1, 0), piece(color, 0, 1, 0), r)
-        send((color, 2, "p0"), piece(color, 0, 1, 0), to(color, 0, 1))
-        r = got((color, 2, "om"))
-        merge(piece(color, 0, 3, 1), piece(color, 0, 3, 1), r)
-        send((color, 2, "m1"), piece(color, 0, 3, 1), to(color, 0, -1))
-    for color in (0, 1):
-        for half in (0, 1):
-            p = got((color, 2, "p%d" % half))
-            m = got((color, 2, "m%d" % half))
-            own = piece(color, 0, 0, half)
-            merge(own, own, p, m)
-            lanes = own.shape[1]
-            for g in range(lanes // HD):
-                col = half * lanes + g * HD
-                out_ref[color * BLK:(color + 1) * BLK, col:col + HD] = own[0:HD, g * HD:(g + 1) * HD].T
+                send((k, h, "m0"), piece(k, h, 0, 3, 0), to(h, 0, -1))
+
+    def second_sums(k):
+        for h in (0, 1):
+            r = got((k, h, "op"))
+            merge(piece(k, h, 0, 1, 0), piece(k, h, 0, 1, 0), r)
+            send((k, h, "p0"), piece(k, h, 0, 1, 0), to(h, 0, 1))
+            r = got((k, h, "om"))
+            merge(piece(k, h, 0, 3, 1), piece(k, h, 0, 3, 1), r)
+            send((k, h, "m1"), piece(k, h, 0, 3, 1), to(h, 0, -1))
+
+    def last_sums(k):
+        for h in (0, 1):
+            for q in (1, 0):
+                p = got((k, h, "p%d" % q))
+                m = got((k, h, "m%d" % q))
+                own = piece(k, h, 0, 0, q)
+                merge(own, own, p, m)
+                for g in range(quart // HD):
+                    col = (h * 2 + q) * quart + g * HD
+                    att[k, :, col:col + HD] = own[0:HD, g * HD:(g + 1) * HD].T
+
+    half = BLK // 2
+    lo, hi = pl.ds(0, half), pl.ds(half, half)
+
+    def ring_of(k):
+        n = k * 4
+        return [
+            remote(att.at[k], attz.at[k, 3], a_send.at[n], a_recv.at[n], zp),
+            remote(att.at[k], attz.at[k, 1], a_send.at[n + 1], a_recv.at[n + 1], zm),
+            remote(attz.at[k, 3, lo], attz.at[k, 2, lo], a_send.at[n + 2], a_recv.at[n + 2], zp),
+            remote(attz.at[k, 1, hi], attz.at[k, 2, hi], a_send.at[n + 3], a_recv.at[n + 3], zm),
+        ]
+
+    def spread_of(k, src):
+        n = k * 6
+        return [
+            remote(src, hb.at[k, 3], b_send.at[n], b_recv.at[n], yp),
+            remote(src, hb.at[k, 1], b_send.at[n + 1], b_recv.at[n + 1], ym),
+            remote(src.at[lo], relay.at[k, 0], b_send.at[n + 2], b_recv.at[n + 2], yp),
+            remote(src.at[hi], relay.at[k, 1], b_send.at[n + 3], b_recv.at[n + 3], ym),
+            remote(relay.at[k, 0], hb.at[k, 2, lo], b_send.at[n + 4], b_recv.at[n + 4], yp),
+            remote(relay.at[k, 1], hb.at[k, 2, hi], b_send.at[n + 5], b_recv.at[n + 5], ym),
+        ]
+
+    def spread(k, dz):
+        src = att.at[k] if dz == 0 else attz.at[k, dz]
+        d = (dz - y + 4) % 4
+
+        @pl.when(d == 0)
+        def _():
+            hb[k, 0] = src[...]
+
+        @pl.when(d == 1)
+        def _():
+            spread_of(k, src)[0].start()
+
+        @pl.when(d == 3)
+        def _():
+            spread_of(k, src)[1].start()
+
+        @pl.when(d == 2)
+        def _():
+            spread_of(k, src)[2].start()
+            spread_of(k, src)[3].start()
+
+    def rows_out(k):
+        r = ring_of(k)
+        r[0].start()
+        r[1].start()
+        spread(k, 0)
+
+    def rows_next(k):
+        r = ring_of(k)
+        r[0].wait_recv()
+        r[2].start()
+        spread(k, 3)
+        r[1].wait_recv()
+        r[3].start()
+        spread(k, 1)
+
+    def rows_far(k):
+        r = ring_of(k)
+        r[2].wait_recv()
+        r[3].wait_recv()
+        spread(k, 2)
+
+    def rows_relay(k):
+        sp = spread_of(k, att.at[k])
+        for n in (0, 1):
+            sp[2 + n].wait_recv()
+            sp[4 + n].start()
+
+    cols = wo_ref.shape[1]
+    width = cols // NCH
+
+    def term(k, r, first):
+        def one(n, carry):
+            sl = pl.ds(pl.multiple_of(n * 256, 256), 256)
+            v = jnp.dot(hb[k, r], w[r, :, sl], preferred_element_type=F32)
+            acc[k, :, sl] = v if first else acc[k, :, sl] + v
+            return carry
+        lax.fori_loop(0, cols // 256, one, 0)
+
+    def terms(k):
+        sp = spread_of(k, att.at[k])
+        if k == 0:
+            w_loads[0].wait()
+        term(k, 0, True)
+        sp[0].wait_recv()
+        if k == 0:
+            w_loads[2].wait()
+        term(k, 3, False)
+        sp[1].wait_recv()
+        if k == 0:
+            w_loads[1].wait()
+        term(k, 1, False)
+        sp[4].wait_recv()
+        sp[5].wait_recv()
+
+    def region(k, f, ch, rows=None):
+        sl = pl.ds(pl.multiple_of(((f + 8) % 4) * cols + ch * width, width), width)
+        first, size = (k * BLK, BLK) if rows is None else (k * BLK + rows * half, half)
+        return out_ref.at[pl.ds(first, size), sl]
+
+    def shifts(k, ch):
+        n = (k * NCH + ch) * 5
+        src = tile.at[k, ch]
+        return [
+            remote(src, region(k, z, ch), s_send.at[n], s_recv.at[n], zp),
+            remote(src, region(k, z, ch), s_send.at[n], s_recv.at[n], zm),
+            remote(src.at[lo], zrelay.at[k, ch, 0], s_send.at[n + 1], s_recv.at[n + 1], zp),
+            remote(src.at[hi], zrelay.at[k, ch, 1], s_send.at[n + 2], s_recv.at[n + 2], zm),
+            remote(zrelay.at[k, ch, 0], region(k, z - 1, ch, 0), s_send.at[n + 3], s_recv.at[n + 3], zp),
+            remote(zrelay.at[k, ch, 1], region(k, z + 1, ch, 1), s_send.at[n + 4], s_recv.at[n + 4], zm),
+        ]
+
+    def home(k, ch):
+        return pltpu.make_async_copy(tile.at[k, ch], region(k, z, ch), home_sem.at[k * NCH + ch])
+
+    def bcast(k, ch):
+        n = (k * NCH + ch) * 4
+        mine = region(k, z - y, ch)
+        up = region(k, z - y + 1, ch, 0)
+        down = region(k, z - y - 1, ch, 1)
+        return [
+            remote(mine, mine, t_send.at[n], t_recv.at[n], yp),
+            remote(mine, mine, t_send.at[n + 1], t_recv.at[n + 1], ym),
+            remote(up, up, t_send.at[n + 2], t_recv.at[n + 2], yp),
+            remote(down, down, t_send.at[n + 3], t_recv.at[n + 3], ym),
+        ]
+
+    def tile_out(k, ch):
+        for n in range(width // 256):
+            sl = slice(ch * width + n * 256, ch * width + (n + 1) * 256)
+            v = acc[k, :, sl] + jnp.dot(hb[k, 2], w[2, :, sl], preferred_element_type=F32)
+            tile[k, ch, :, n * 256:(n + 1) * 256] = v.astype(BF16)
+
+        @pl.when(y == 0)
+        def _():
+            home(k, ch).start()
+
+        @pl.when(y == 1)
+        def _():
+            shifts(k, ch)[0].start()
+
+        @pl.when(y == 3)
+        def _():
+            shifts(k, ch)[1].start()
+
+        @pl.when(y == 2)
+        def _():
+            shifts(k, ch)[2].start()
+            shifts(k, ch)[3].start()
+
+    def tile_relay(k, ch):
+        @pl.when(y == 2)
+        def _():
+            sr = shifts(k, ch)
+            sr[2].wait_recv()
+            sr[4].start()
+            sr[3].wait_recv()
+            sr[5].start()
+
+    def tile_home(k, ch):
+        @pl.when(y == 0)
+        def _():
+            home(k, ch).wait()
+
+        @pl.when(y % 2 == 1)
+        def _():
+            shifts(k, ch)[0].wait_recv()
+
+        @pl.when(y == 2)
+        def _():
+            se = shifts(k, ch)
+            se[4].wait_recv()
+            se[5].wait_recv()
+
+        b = bcast(k, ch)
+        b[0].start()
+        b[1].start()
+
+    def tile_onward(k, ch):
+        b = bcast(k, ch)
+        b[0].wait_recv()
+        b[2].start()
+        b[1].wait_recv()
+        b[3].start()
+
+    for b in SECOND:
+        first_sends(0, b)
+    for b in SECOND:
+        first_raw(0, b)
+    for b in SECOND:
+        first_sums(0, b)
+    for b in SECOND:
+        first_sends(1, b)
+        second_sends(0, b)
+    for n in (0, 1):
+        wo_copies[n].wait_recv()
+        send_wo(w.at[2], 2 + n, partner)
+    second_sums(0)
+    for b in SECOND:
+        first_raw(1, b)
+    last_sums(0)
+    rows_out(0)
+    for b in SECOND:
+        first_sums(1, b)
+    rows_next(0)
+    second_sends(1, 2)
+    second_sends(1, 1)
+    rows_far(0)
+    second_sends(1, 3)
+    second_sends(1, 0)
+    rows_relay(0)
+    second_sums(1)
+    terms(0)
+    last_sums(1)
+    rows_out(1)
+    wo_copies[2].wait_recv()
+    wo_copies[3].wait_recv()
+    for ch in range(NCH):
+        tile_out(0, ch)
+    rows_next(1)
+    for ch in range(NCH):
+        tile_relay(0, ch)
+    tile_home(0, 0)
+    tile_home(0, 1)
+    rows_far(1)
+    tile_home(0, 2)
+    tile_home(0, 3)
+    rows_relay(1)
+    tile_onward(0, 0)
+    terms(1)
+    for ch in range(NCH):
+        tile_out(1, ch)
+    tile_onward(0, 1)
+    tile_onward(0, 2)
+    tile_onward(0, 3)
+    for t in range(NCH + 2):
+        if t < NCH:
+            tile_relay(1, t)
+        if 1 <= t < NCH + 1:
+            tile_home(1, t - 1)
+        if 2 <= t:
+            tile_onward(1, t - 2)
+    for k in (0, 1):
+        for ch in range(NCH):
+            b = bcast(k, ch)
+            b[2].wait_recv()
+            b[3].wait_recv()
+            for cp in b:
+                cp.wait_send()
+
+            @pl.when(y % 2 == 1)
+            def _():
+                shifts(k, ch)[0].wait_send()
+
+            @pl.when(y == 2)
+            def _():
+                for cp in shifts(k, ch)[2:]:
+                    cp.wait_send()
+        for cp in ring_of(k) + spread_of(k, att.at[k]):
+            cp.wait_send()
+    for cp in wo_copies:
+        cp.wait_send()
     for cp, _ in copies.values():
         cp.wait_send()
 
 
-N_REDUCE = 60
-
-
-def reduce_partials(part):
+N_REDUCE = 120
+
+
+def finish(part, wo, won):
     rows, lanes = part.shape[-2:]
+    depth, cols = wo.shape
+    anyspec = pl.BlockSpec(memory_space=pl.ANY)
+    sem = pltpu.SemaphoreType.DMA
     return pl.pallas_call(
-        reduce_kernel,
-        out_shape=jax.ShapeDtypeStruct((2 * BLK, 2 * lanes), BF16),
-        in_specs=[pl.BlockSpec(memory_space=pl.ANY)],
-        out_specs=pl.BlockSpec(memory_space=pltpu.VMEM),
+        finish_kernel,
+        out_shape=jax.ShapeDtypeStruct((2 * BLK, 4 * cols), BF16),
+        in_specs=[anyspec] * 3,
+        out_specs=anyspec,
         scratch_shapes=[
-            pltpu.VMEM((2, 16, 2, rows, lanes), BF16),
-            pltpu.VMEM((N_REDUCE, rows, lanes), BF16),
-            pltpu.SemaphoreType.DMA((N_REDUCE,)),
-            pltpu.SemaphoreType.DMA((N_REDUCE,)),
-            pltpu.SemaphoreType.DMA((32,)),
+            pltpu.VMEM((4, 16, rows, lanes), BF16),
+            pltpu.VMEM((N_REDUCE, rows, lanes // 2), BF16),
+            pltpu.VMEM((2, BLK, depth), BF16),
+            pltpu.VMEM((2, 4, BLK, depth), BF16),
+            pltpu.VMEM((2, 4, BLK, depth), BF16),
+            pltpu.VMEM((2, 2, BLK // 2, depth), BF16),
+            pltpu.VMEM((4, depth, cols), BF16),
+            pltpu.VMEM((2, BLK, cols), F32),
+            pltpu.VMEM((2, NCH, BLK, cols // NCH), BF16),
+            pltpu.VMEM((2, NCH, 2, BLK // 2, cols // NCH), BF16),
+            sem((64,)), sem((N_REDUCE,)), sem((N_REDUCE,)), sem((4,)), sem((4,)), sem((3,)),
+            sem((8,)), sem((8,)), sem((12,)), sem((12,)),
+            sem((10 * NCH,)), sem((10 * NCH,)), sem((8 * NCH,)), sem((8 * NCH,)), sem((2 * NCH,)),
         ],
         compiler_params=pltpu.CompilerParams(
-            collective_id=1, has_side_effects=True, vmem_limit_bytes=40 * 2**20),
-        name="reduce_partials",
-    )(part)
+            collective_id=1, has_side_effects=True, vmem_limit_bytes=VMEM),
+        name="finish",
+    )(part, wo, won)
+
+
+def turn_kernel(q_ref, out_ref):
+    for color in range(2):
+        for g in range(q_ref.shape[1] // HD):
+            out_ref[color, :, g * BLK:(g + 1) * BLK] = q_ref[color * BLK:(color + 1) * BLK, g * HD:(g + 1) * HD].T
+
+
+def turn(queries):
+    return pl.pallas_call(
+        turn_kernel,
+        out_shape=jax.ShapeDtypeStruct((2, HD, queries.shape[1]), BF16),
+        in_specs=[pl.BlockSpec(memory_space=pltpu.VMEM)],
+        out_specs=pl.BlockSpec(memory_space=pltpu.VMEM),
+        compiler_params=pltpu.CompilerParams(vmem_limit_bytes=VMEM),
+        name="turn",
+    )(queries)
 
 
 def request_table(block_slot, pattern, core, cb_local):
@@ -456,14 +802,10 @@
 def body(queries, span_k, span_v, cache_k, cache_v, block_slot, pattern, wo):
     core = lax.axis_index("seq") % 2
     tab = request_table(block_slot, pattern, core, cache_k.shape[0])
-    q = queries.reshape(2, BLK, queries.shape[1])
-    q_all, pk, pv, prev, tab_all = gather_queries(q, cache_k, cache_v, span_k, span_v, tab)
+    q = turn(queries)
+    q_all, pk, pv, prev, tab_all, won = gather_queries(q, cache_k, cache_v, span_k, span_v, tab, wo)
     part = attend(tab_all, q_all, cache_k, cache_v, pk, pv, span_k, span_v, prev)
-    attended = reduce_partials(part)
-    partial_terms = jnp.dot(
-        attended, lax.all_gather(wo, "fsdp", axis=1, tiled=True), preferred_element_type=F32
-    )
-    return lax.psum(partial_terms.astype(BF16), "head")
+    return finish(part, wo, won)
 
 
 def solution(mesh):

time: 361 us -> 266 us (0.74)
  waiting for transfers between devices: 92.3 us -> 0 us
  Pallas kernels: 225 us -> 258 us
  between operations: 13.6 us -> 0.07 us
  matrix products: 11.9 us -> 0 us
  local copies, waits for them, and re-layouts: 16.8 us -> 6.65 us
    psum x1 -> x0, waiting for transfers between devices: 91.6 us -> none  [body(): return lax.psum(partial_terms.astype(BF16), 'head')]
    pallas_call x1 -> x2, Pallas kernels: 65 us -> 146 us  [the longest x1 144 us: finish(): pl.pallas_call(finish_kernel, out_shape=jax.ShapeDtypeStruct((2 * BLK, 4...]
    pallas_call x1, Pallas kernels: 74 us -> 48.4 us  [attend(): pl.pallas_call(attend_kernel, out_shape=jax.ShapeDtypeStruct((16, 2, 2, H...]
    pallas_call x1, Pallas kernels: 85.7 us -> 63.6 us  [gather_queries(): pl.pallas_call(gather_kernel, out_shape=(jax.ShapeDtypeStruct((16, 2, BLK...]
    dot_general x1 -> x0, matrix products: 11.9 us -> none  [body(): jnp.dot(attended, lax.all_gather(wo, 'fsdp', axis=1, tiled=True), preferr...]
    unnamed x23 -> x3, local copies, waits for them, and re-layouts: 14.8 us -> 4.64 us
  transfers between devices with their start and end apart: 2 -> 0, of which waited for: 1 -> 0; matrix products, arithmetic and copies ran while one was open for 1% -> 0% of each run, Pallas kernels for 62% -> 0%
where the time goes in v3:
time: 266 us
  Pallas kernels  258 us (97%)
  local copies, waits for them, and re-layouts  6.65 us (2%)
    pallas_call x1, Pallas kernels, finish(): pl.pallas_call(finish_kernel, out_shape=jax.ShapeDtypeStruct((2 * BLK, 4...  144 us
    pallas_call x1, Pallas kernels, gather_queries(): pl.pallas_call(gather_kernel, out_shape=(jax.ShapeDtypeStruct((16, 2, BLK...  63.6 us
    pallas_call x1, Pallas kernels, attend(): pl.pallas_call(attend_kernel, out_shape=jax.ShapeDtypeStruct((16, 2, 2, H...  48.4 us

profile of v3, /device:TPU:0, one launch (start us, length us, event | category | flops | bytes accessed | tf_op | source)
XLA Modules:
  0.0 266.1 jit_solution(15819172378005636689)
XLA Ops:
  0.0 0.0 copy-start
  0.0 0.7 compare_select_fusion
  0.7 0.1 reshape.164
  0.8 0.0 copy-done
  0.8 1.1 gather_fusion
  1.9 0.1 reshape.163
  2.1 0.2 convert_reduce_fusion
  2.3 0.7 select_reduce_fusion
  3.0 0.1 reshape.161
  3.1 0.6 pad.4.tab_ref
  3.7 2.0 turn.1.q_ref
  5.7 63.6 %gather_queries.1 = (bf16[16,2,128,1024]{3,2,1,0:T(8,128)(2,1)}, bf16[64,128,128]{2,1,0:T(8,128)(2,1)}, bf16[64,128,128]{2,1,0:T(8,128)(2,1)}, bf16[2,128,128]{2...) custom-call(bf16[2,128,1024]{2,1,0:T(8,128)(2,1)} %turn.1.q_ref, bf16[64,128,128]{2,1,0:T(8,128)(2,1)} %ck_ref.3, ...), custom_call_target="tpu_custom_call" | custom-call | tf_op jit(solution)/shard_map/gather_queries/pallas_call | solution.py:155
  69.4 48.4 %attend.1.part_ref = bf16[16,2,2,144,512]{4,3,2,1,0:T(8,128)(2,1)} custom-call(s32[16,1,128]{2,1,0:T(1,128)} %get-tuple-element.11.tab_ref, bf16[16,2,128,1024]{3,2,1,0:T(8,128)(2,1)} %get-tuple-element.12.q_ref, bf16[64,128,128]{2,1,0:T(8,128)(2,1)} %ck_ref.3, bf16[64,128,128]{2,1,0:T(8,128)(2,1)} %cv_ref.3, ...), custom_call_target="tpu_custom_call" | custom-call | flops 7000000000 | bytes 26000000 | tf_op jit(solution)/shard_map/attend/pallas_call | solution.py:278
  117.8 143.7 %finish.1 = bf16[256,8192]{1,0:T(8,128)(2,1)} custom-call(bf16[16,2,2,144,512]{4,3,2,1,0:T(8,128)(2,1)} %attend.1.part_ref, bf16[1024,2048]{1,0:T(8,128)(2,1)} %wo_ref.3, bf16[2,1024,2048]{2,1,0:T(8,128)(2,1)} %get-tuple-element.16.won_ref), custom_call_target="tpu_custom_call" | custom-call | tf_op jit(solution)/shard_map/finish/pallas_call | solution.py:743
  261.5 4.6 %copy.10 = bf16[256,8192]{1,0:T(8,128)(2,1)} copy(bf16[256,8192]{1,0:T(8,128)(2,1)} %finish.1) | data formatting | bytes 8388608
  (7 shorter events, 0.1 us)
Async XLA Ops:
  0.0 0.8 copy-start
